TPU v7x, 128 devices: a whole 4x4x4 slice. The times are simulated.
128 devices in a mesh: wide: 64 (over y, z_lo, x, core), narrow: 2 (over z_hi).
Axes of the slice: x: 4, y: 4, z: 4 (z_hi: 2, z_lo: 2; z = z_hi * 2 + z_lo), core: 2. Of those that a mesh axis runs over, the one named last changes fastest.
Arguments:
- voltages: bfloat16 [512, 1048576], P('wide', 'narrow'), may hold values from -6 to 6
- following: bfloat16 [512, 30720], P('wide'), may hold values from -6 to 6
Outputs:
- visibilities: float32 [1024, 2, 512, 512], P(('wide', 'narrow'))
All inputs are finite; a program needn't handle non-finite values.
Results may differ from a plain program's by a relative error of at most 0.0028.
Values may be sent and summed in bfloat16 or wider, within the bound.
A program may use at most 192 MiB of HBM per device.

v0:
```python
import math

import jax
import jax.numpy as jnp
from jax import lax
from jax.sharding import PartitionSpec as P

FFT_LEN = 2048
CHANNELS = 1024
TAPS = 16


def from_behind(x, axis, by):
    size = lax.axis_size(axis)
    pairs = [(i, i + by) for i in range(size) if 0 <= i + by < size]
    return lax.ppermute(x, axis, pairs)


def pfb_window(block_len, tap_count):
    length_all = tap_count * block_len
    sample_pos = jnp.arange(length_all, dtype=jnp.float32)
    centred = (sample_pos + 0.5 - length_all / 2.0) / block_len
    taper = 0.5 - 0.5 * jnp.cos(2.0 * jnp.pi * (sample_pos + 0.5) / length_all)
    return jnp.sinc(centred) * taper


def phase_table(first_len, second_len, modulus):
    first_idx = jnp.arange(first_len, dtype=jnp.int32)[:, None]
    second_idx = jnp.arange(second_len, dtype=jnp.int32)[None, :]
    turns = (first_idx * second_idx % modulus).astype(jnp.float32)
    angles = 2.0 * jnp.pi * turns / modulus
    return (jnp.cos(angles), jnp.sin(angles))


def shards(voltages, following):
    local_inputs, local_span = voltages.shape
    local_spec = local_span // FFT_LEN
    halo_len = (TAPS - 1) * FFT_LEN
    leading = voltages[:, :halo_len]
    shifted = from_behind(leading, "narrow", -1)
    is_final = lax.axis_index("narrow") == lax.axis_size("narrow") - 1
    after_rows = jnp.where(is_final, following, shifted)
    samples = jnp.concatenate([voltages, after_rows], axis=1)
    samples = samples.reshape(local_inputs, local_spec + TAPS - 1, FFT_LEN)
    blocks = jnp.transpose(samples, (2, 0, 1))
    weights_taps = pfb_window(FFT_LEN, TAPS).reshape(TAPS, FFT_LEN)
    filtered = jnp.zeros((FFT_LEN, local_inputs, local_spec), jnp.float32)
    for tap_index in range(TAPS):
        filtered = filtered + weights_taps[tap_index][:, None, None] * blocks[
            :, :, tap_index : tap_index + local_spec
        ].astype(jnp.float32)
    bit_count = FFT_LEN.bit_length() - 1
    outer_len = 2 ** (bit_count // 2)
    inner_len = FFT_LEN // outer_len
    kept_len = inner_len // 2
    row_count = local_inputs * local_spec
    folded = filtered.reshape(outer_len, inner_len, row_count)
    highest = lax.Precision.HIGHEST
    cos_outer, sin_outer = phase_table(outer_len, outer_len, outer_len)
    first_real = jnp.einsum("abr,ac->cbr", folded, cos_outer, precision=highest)
    first_imag = -jnp.einsum("abr,ac->cbr", folded, sin_outer, precision=highest)
    cos_twiddle, sin_twiddle = phase_table(outer_len, inner_len, FFT_LEN)
    cos_twiddle = cos_twiddle[:, :, None]
    sin_twiddle = sin_twiddle[:, :, None]
    turned_real = first_real * cos_twiddle + first_imag * sin_twiddle
    turned_imag = first_imag * cos_twiddle - first_real * sin_twiddle
    cos_inner, sin_inner = phase_table(inner_len, kept_len, inner_len)
    final_real = jnp.einsum("cbr,bd->dcr", turned_real, cos_inner, precision=highest) + jnp.einsum(
        "cbr,bd->dcr", turned_imag, sin_inner, precision=highest
    )
    final_imag = jnp.einsum("cbr,bd->dcr", turned_imag, cos_inner, precision=highest) - jnp.einsum(
        "cbr,bd->dcr", turned_real, sin_inner, precision=highest
    )
    scaling = 1.0 / math.sqrt(FFT_LEN)
    final_real = final_real.reshape(CHANNELS, local_inputs, local_spec) * scaling
    final_imag = final_imag.reshape(CHANNELS, local_inputs, local_spec) * scaling
    spectra = jnp.stack([final_real, final_imag], axis=1).astype(jnp.bfloat16)
    gathered = lax.all_to_all(
        lax.all_to_all(spectra, "wide", split_axis=0, concat_axis=2, tiled=True),
        "narrow",
        split_axis=0,
        concat_axis=3,
        tiled=True,
    )
    chan_dev = gathered.shape[0]
    all_inputs = gathered.shape[2]
    time_len = gathered.shape[3]
    stacked = gathered.reshape(chan_dev, 2 * all_inputs, time_len)
    gram = lax.dot_general(
        stacked, stacked, (((2,), (2,)), ((0,), (0,))), preferred_element_type=jnp.float32
    )
    vis_real = gram[:, :all_inputs, :all_inputs] + gram[:, all_inputs:, all_inputs:]
    vis_imag = gram[:, all_inputs:, :all_inputs] - gram[:, :all_inputs, all_inputs:]
    return jnp.stack([vis_real, vis_imag], axis=1) / time_len


def solution(mesh):
    in_specs = (P("wide", "narrow"), P("wide", None))
    out_specs = P(("wide", "narrow"), None, None, None)
    return jax.shard_map(shards, mesh=mesh, in_specs=in_specs, out_specs=out_specs, check_vma=False)
```

profile of v0, /device:TPU:1, one launch (start us, length us, event | category | flops | bytes accessed | tf_op | source)
XLA Modules:
  0.0 653.0 jit_solution(1256518711793317111)
XLA Ops:
  0.0 1.1 slice.128
  1.1 1.3 collective-permute-start
  2.4 0.6 fusion.22
  3.0 0.1 fusion.66
  3.2 14.3 %collective-permute-done = bf16[8,30720]{1,0:T(8,128)(2,1)S(1)} collective-permute-done((bf16[8,30720]{1,0:T(8,128)(2,1)S(1)}, bf16[8,30720]{1,0:T(8,128)(2,1)S(1)}, u32[]{:S(2)}, u32[]{:S(2)}) %collective-permute-start) | collective-permute-done | bytes 491552 | tf_op jit(solution)/shard_map/ppermute | solution.py:16
  17.5 0.1 broadcast_select_fusion
  17.6 21.3 %pad_maximum_fusion = bf16[8,555008]{1,0:T(8,128)(2,1)} fusion(bf16[8,30720]{1,0:T(8,128)(2,1)S(1)} %broadcast_select_fusion, bf16[8,524288]{1,0:T(8,128)(2,1)} %param.2), kind=kLoop, calls=%fused_computation.16 | loop fusion | flops 17760256 | bytes 17760256 | tf_op jit(solution)/shard_map/concatenate | solution.py:43
  38.9 16.6 %copy.32 = bf16[8,271,2048]{1,0,2:T(8,128)(2,1)} copy(bf16[8,271,2048]{2,0,1:T(8,128)(2,1)} %bitcast.46) | data formatting | bytes 17760256 | tf_op jit(solution)/shard_map/reshape | solution.py:44
  55.5 108.2 %multiply_add_fusion.1 = f32[2048,8,256]{2,1,0:T(8,128)} fusion(bf16[2048,8,271]{2,1,0:T(8,128)(2,1)} %bitcast.45, f32[2048]{0:T(1024)S(1)} %get-tuple-element.10, f32[2048]{0:T(1024)S(1)} %get-tuple-element.11, f32[2048]{0:T(1024)S(1)} %get-tuple-element.12, f32[2048]{0:T(1024)S(1)} %get-tuple-element.13, f32[2048]{0:T(1024)S(1)} %get-tuple-element.14, ...), kind=kLoop, calls=%fused_computation.3 | loop fusion | flops 197132288 | bytes 151126016 | tf_op jit(solution)/shard_map/add | solution.py:49
  163.6 18.0 %reshape.124 = f32[32,64,2048]{2,1,0:T(8,128)} reshape(f32[2048,8,256]{2,1,0:T(8,128)} %multiply_add_fusion.1) | data formatting | bytes 33554432 | tf_op jit(solution)/shard_map/reshape | solution.py:57
  181.6 33.0 %fusion.8 = f32[32,64,2048]{2,0,1:T(8,128)} fusion(f32[32,64,2048]{2,1,0:T(8,128)} %reshape.124), kind=kOutput, calls=%fused_computation.12 | convolution fusion | flops 1610627072 | bytes 33554432 | tf_op jit(solution)/shard_map/abr,ac->cbr/dot_general | solution.py:61
  214.6 34.5 %multiply_add_fusion = (f32[32,64,2048]{2,0,1:T(8,128)}, f32[32,64,2048]{2,0,1:T(8,128)S(1)}) fusion(f32[32,64,2048]{2,0,1:T(8,128)} %fusion.8, f32[32,64]{0,1:T(8,128)S(1)} %get-tuple-element.25, f32[32,64]{0,1:T(8,128)S(1)} %get-tuple-element.26, f32[32,64,2048]{2,1,0:T(8,128)} %reshape.124), kind=kOutput, calls=%fused_computation.2 | convolution fusion | flops 1639987200 | bytes 67125248 | tf_op jit(solution)/shard_map/abr,ac->cbr/dot_general | solution.py:60
  249.1 19.0 %fusion = f32[32,32,2048]{2,0,1:T(8,128)} fusion(f32[32,64,2048]{2,0,1:T(8,128)S(1)} %get-tuple-element.6), kind=kOutput, calls=%fused_computation.4 | convolution fusion | flops 1610641408 | bytes 25165824 | tf_op jit(solution)/shard_map/cbr,bd->dcr/dot_general | solution.py:71
  268.1 18.8 %fusion.2 = f32[32,32,2048]{2,0,1:T(8,128)} fusion(f32[32,64,2048]{2,0,1:T(8,128)S(1)} %get-tuple-element.6), kind=kOutput, calls=%fused_computation.6 | convolution fusion | flops 1610641408 | bytes 25165824 | tf_op jit(solution)/shard_map/cbr,bd->dcr/dot_general | solution.py:68
  286.9 0.0 slice-start
  287.0 0.0 slice-start.1
  287.0 26.5 %multiply_convert_fusion.1 = bf16[32,32,2048]{2,0,1:T(8,128)(2,1)S(1)} fusion(f32[32,32,2048]{2,0,1:T(8,128)} %fusion.2, f32[32,64,2048]{2,0,1:T(8,128)} %get-tuple-element.5), kind=kOutput, calls=%fused_computation.24 | convolution fusion | flops 1616932864 | bytes 29360128 | tf_op jit(solution)/shard_map/cbr,bd->dcr/dot_general | solution.py:68
  313.5 0.0 slice-done
  313.5 0.0 slice-done.1
  313.5 26.4 %multiply_convert_fusion = bf16[32,32,2048]{2,0,1:T(8,128)(2,1)} fusion(f32[32,32,2048]{2,0,1:T(8,128)S(1)} %bitcast.48, f32[32,64,2048]{2,0,1:T(8,128)} %get-tuple-element.5), kind=kOutput, calls=%fused_computation.23 | convolution fusion | flops 1616932864 | bytes 29360128 | tf_op jit(solution)/shard_map/cbr,bd->dcr/dot_general | solution.py:71
  339.9 4.5 copy.40
  344.4 3.4 copy.46
  347.8 2.3 copy.37
  350.1 1.5 copy.45
  351.6 6.4 pad_maximum_fusion.1
  357.9 7.3 %copy.41 = bf16[1024,2,8,256]{3,2,1,0:T(8,128)(2,1)} copy(bf16[1024,2,8,256]{3,2,0,1:T(8,128)(2,1)} %pad_maximum_fusion.1) | data formatting | bytes 16777216 | tf_op jit(solution)/shard_map/stack | solution.py:77
  365.2 107.1 %all_to_all.33 = bf16[1024,2,8,256]{3,2,1,0:T(8,128)(2,1)} all-to-all(bf16[1024,2,8,256]{3,2,1,0:T(8,128)(2,1)} %copy.41), channel_id=1, replica_groups=mesh['wide'=64,'narrow'=2] {'wide'}, dimensions={0} | all-to-all | bytes 16777216 | tf_op jit(solution)/shard_map/all_to_all | solution.py:79
  472.4 7.8 %copy.66 = bf16[16,2,64,8,256]{4,3,2,1,0:T(8,128)(2,1)} copy(bf16[16,2,64,8,256]{4,3,1,0,2:T(8,128)(2,1)} %bitcast.49) | data formatting | bytes 16777216 | tf_op jit(solution)/shard_map/all_to_all | solution.py:79
  480.2 98.8 %all_to_all.34 = bf16[16,2,512,256]{3,2,1,0:T(8,128)(2,1)S(1)} all-to-all(bf16[16,2,512,256]{3,2,1,0:T(8,128)(2,1)} %bitcast.50), channel_id=1, replica_groups=mesh['wide'=64,'narrow'=2] {'narrow'}, dimensions={0} | all-to-all | bytes 16777216 | tf_op jit(solution)/shard_map/all_to_all | solution.py:78
  578.9 7.7 %copy.43 = bf16[8,2,512,2,256]{4,3,2,1,0:T(2,128)(2,1)} copy(bf16[8,2,512,2,256]{4,2,1,0,3:T(8,128)(2,1)S(1)} %bitcast.51) | data formatting | bytes 16777216 | tf_op jit(solution)/shard_map/all_to_all | solution.py:78
  586.6 14.0 %reshape.125 = bf16[8,1024,512]{2,1,0:T(8,128)(2,1)} reshape(bf16[8,2,512,2,256]{4,3,2,1,0:T(2,128)(2,1)} %copy.43) | data formatting | bytes 16777216 | tf_op jit(solution)/shard_map/reshape | solution.py:88
  600.6 19.2 %fusion.108 = f32[8,1024,1024]{2,1,0:T(8,128)} fusion(bf16[8,1024,512]{2,1,0:T(8,128)(2,1)} %reshape.125), kind=kOutput, calls=%fused_computation.127 | convolution fusion | flops 8589934592 | bytes 41943040 | tf_op jit(solution)/shard_map/dot_general | solution.py:89
  619.8 19.1 %fusion.13 = (f32[8,1,512,512]{3,2,0,1:T(8,128)}, f32[8,1,512,512]{3,2,0,1:T(8,128)}) fusion(f32[8,1024,1024]{2,1,0:T(8,128)} %fusion.108), kind=kLoop, calls=%fused_computation.20 | loop fusion | flops 4194304 | bytes 50331648 | tf_op jit(solution)/shard_map/stack | solution.py:94
  639.0 7.4 %maximum_multiply_fusion = f32[8,2,512,512]{3,2,0,1:T(8,128)S(1)} fusion(f32[8,1,512,512]{3,2,0,1:T(8,128)} %get-tuple-element.8, f32[8,1,512,512]{3,2,0,1:T(8,128)} %get-tuple-element.7), kind=kLoop, calls=%fused_computation | loop fusion | flops 8388608 | bytes 33554432 | tf_op jit(solution)/shard_map/div | solution.py:94
  646.4 6.4 copy.44
  (2 shorter events, 0.0 us)
Async XLA Ops:
  1.1 16.4 %collective-permute-start = (bf16[8,30720]{1,0:T(8,128)(2,1)S(1)}, bf16[8,30720]{1,0:T(8,128)(2,1)S(1)}, u32[]{:S(2)}, u32[]{:S(2)}) collective-permute-start(bf16[8,30720]{1,0:T(8,128)(2,1)S(1)} %slice.128), channel_id=1, source_target_pairs={{1,0},{3,2},{5,4},{7,6},{9,8},{11,10},{13,12},{15,14},{17,16},{19,... | collective-permute-start | bytes 1474568 | tf_op jit(solution)/shard_map/ppermute | solution.py:16
  286.9 26.5 %slice-start = ((s8[8388608]{0:T(1024)(128)(4,1)}), s8[4194304]{0:T(1024)(128)(4,1)S(1)}, s32[]{:S(2)}) async-start(s8[8388608]{0:T(1024)(128)(4,1)} %bitcast.47), calls=%async_computation.2 | async-start | bytes 8388608
  287.0 26.5 %slice-start.1 = ((s8[8388608]{0:T(1024)(128)(4,1)}), s8[4194304]{0:T(1024)(128)(4,1)S(1)}, s32[]{:S(2)}) async-start(s8[8388608]{0:T(1024)(128)(4,1)} %bitcast.47), calls=%async_computation.3 | async-start | bytes 8388608
where the time goes:
time: 660 us; the launch traced here: 653 us
  blocking collectives  206 us (31%)
  matrix products  177 us (27%)
  other arithmetic  163 us (25%)
  local copies, waits for them, and re-layouts  90.5 us (14%)
  waiting for transfers between devices  14.3 us (2%)
    add x1, other arithmetic, shards(): filtered + weights_taps[tap_index][:, None, None] * blocks[:, :, tap_inde...  108 us
    all_to_all x1, blocking collectives, shards(): lax.all_to_all(spectra, 'wide', split_axis=0, concat_axis=2, tiled=True)  107 us
    all_to_all x1, blocking collectives, shards(): lax.all_to_all(lax.all_to_all(spectra, 'wide', split_axis=0, concat_axis=...  98.8 us
    dot_general x1, matrix products, shards(): first_real = jnp.einsum('abr,ac->cbr', folded, cos_outer, precision=highest)  34.5 us
    dot_general x1, matrix products, shards(): jnp.einsum('abr,ac->cbr', folded, sin_outer, precision=highest)  33 us
    dot_general x1, matrix products, shards(): jnp.einsum('cbr,bd->dcr', turned_real, cos_inner, precision=highest)  26.5 us
    dot_general x1, matrix products, shards(): jnp.einsum('cbr,bd->dcr', turned_real, sin_inner, precision=highest)  26.4 us
    concatenate x1, other arithmetic, shards(): samples = jnp.concatenate([voltages, after_rows], axis=1)  21.3 us
  transfers between devices with their start and end apart: 1, of which 1 were waited for; matrix products, arithmetic and copies ran while one was open for 0% of the time, Pallas kernels for 0%

commit v1 on v0

v1 whole, which is shorter than its diff:
```python
import math

import jax
import jax.numpy as jnp
from jax import lax
from jax.sharding import PartitionSpec as P

FFT_LEN = 2048
CHANNELS = 1024
TAPS = 16


def from_behind(x, axis, by):
    size = lax.axis_size(axis)
    pairs = [(i, i + by) for i in range(size) if 0 <= i + by < size]
    return lax.ppermute(x, axis, pairs)


def pfb_window(block_len, tap_count):
    length_all = tap_count * block_len
    sample_pos = jnp.arange(length_all, dtype=jnp.float32)
    centred = (sample_pos + 0.5 - length_all / 2.0) / block_len
    taper = 0.5 - 0.5 * jnp.cos(2.0 * jnp.pi * (sample_pos + 0.5) / length_all)
    return jnp.sinc(centred) * taper


def phase(first_idx, second_idx):
    turns = (first_idx * second_idx % FFT_LEN).astype(jnp.float32)
    angles = (2.0 * jnp.pi / FFT_LEN) * turns
    return jnp.cos(angles), jnp.sin(angles)


def dft_matrix(salt):
    chan = jnp.arange(CHANNELS, dtype=jnp.int32)[None, :] + salt
    hi_c, hi_s = phase(jnp.arange(FFT_LEN // 64, dtype=jnp.int32)[:, None] * 64, chan)
    lo_c, lo_s = phase(jnp.arange(64, dtype=jnp.int32)[:, None], chan)
    cos_t = hi_c[:, None, :] * lo_c[None, :, :] - hi_s[:, None, :] * lo_s[None, :, :]
    sin_t = hi_s[:, None, :] * lo_c[None, :, :] + hi_c[:, None, :] * lo_s[None, :, :]
    scaling = 1.0 / math.sqrt(FFT_LEN)
    table = jnp.concatenate([cos_t * scaling, sin_t * (-scaling)], axis=-1)
    return table.reshape(FFT_LEN, 2 * CHANNELS)


def shards(voltages, following):
    local_inputs, local_span = voltages.shape
    local_spec = local_span // FFT_LEN
    halo_len = (TAPS - 1) * FFT_LEN
    leading = voltages[:, :halo_len]
    shifted = from_behind(leading, "narrow", -1)
    is_final = lax.axis_index("narrow") == lax.axis_size("narrow") - 1
    after_rows = jnp.where(is_final, following, shifted)
    samples = jnp.concatenate([voltages, after_rows], axis=1)
    blocks = samples.reshape(local_inputs, local_spec + TAPS - 1, FFT_LEN).astype(jnp.float32)
    weights_taps = pfb_window(FFT_LEN, TAPS).reshape(TAPS, FFT_LEN)
    filtered = weights_taps[0][None, None, :] * blocks[:, 0:local_spec, :]
    for tap_index in range(1, TAPS):
        filtered = filtered + weights_taps[tap_index][None, None, :] * blocks[
            :, tap_index : tap_index + local_spec, :
        ]
    salt = lax.optimization_barrier(jnp.zeros((), jnp.int32))
    table = dft_matrix(salt)
    rows = filtered.reshape(local_inputs * local_spec, FFT_LEN)
    spec = jnp.einsum("rk,kn->nr", rows, table, precision=lax.Precision.HIGH,
                      preferred_element_type=jnp.float32)
    spec = spec.astype(jnp.bfloat16).reshape(2, CHANNELS, local_inputs, local_spec)
    spec = jnp.transpose(spec, (1, 0, 2, 3))
    got = lax.all_to_all(spec, ("wide", "narrow"), 0, 0, tiled=True)
    n_wide = lax.axis_size("wide")
    n_narrow = lax.axis_size("narrow")
    chan_dev = CHANNELS // (n_wide * n_narrow)
    got = got.reshape(n_wide, n_narrow, chan_dev, 2, local_inputs, local_spec)
    got = jnp.transpose(got, (2, 3, 0, 4, 1, 5))
    all_inputs = n_wide * local_inputs
    time_len = n_narrow * local_spec
    got = got.reshape(chan_dev, 2, all_inputs, time_len)
    re = got[:, 0]
    im = got[:, 1]
    both = jnp.concatenate([re, im], axis=-1)
    turned = jnp.concatenate([im, -re], axis=-1)
    lhs = jnp.stack([both, turned], axis=1)
    vis = jnp.einsum("csik,cjk->csij", lhs, both, preferred_element_type=jnp.float32)
    return vis * (1.0 / time_len)


def solution(mesh):
    in_specs = (P("wide", "narrow"), P("wide", None))
    out_specs = P(("wide", "narrow"), None, None, None)
    return jax.shard_map(shards, mesh=mesh, in_specs=in_specs, out_specs=out_specs, check_vma=False)
```

time: 660 us -> 463 us (0.70)
  blocking collectives: 206 us -> 106 us
  matrix products: 177 us -> 130 us
  local copies, waits for them, and re-layouts: 90.5 us -> 60.1 us
  waiting for transfers between devices: 14.3 us -> 5.01 us
  other arithmetic: 163 us -> 156 us
    all_to_all x2 -> x1, blocking collectives: 206 us -> 106 us  [shards(): got = lax.all_to_all(spec, ('wide', 'narrow'), 0, 0, tiled=True)]
    dot_general x7 -> x2, matrix products: 177 us -> 130 us  [the longest x1 113 us: shards(): jnp.einsum('rk,kn->nr', rows, table, precision=lax.Precision.HIGH, prefer...]
    reshape x3 -> x1, local copies, waits for them, and re-layouts: 48.6 us -> 7.62 us  [shards(): got = got.reshape(n_wide, n_narrow, chan_dev, 2, local_inputs, local_spec)]
    add x0 -> x1, local copies, waits for them, and re-layouts: none -> 29.3 us  [shards(): filtered + weights_taps[tap_index][None, None, :] * blocks[:, tap_index:t...]
    another operation x2 -> x1, other arithmetic: 25.5 us -> 7.96 us  [shards(): lhs = jnp.stack([both, turned], axis=1)]
    all_to_all x2 -> x0, local copies, waits for them, and re-layouts: 15.5 us -> none  [the longest x1 7.81 us: shards(): lax.all_to_all(spectra, 'wide', split_axis=0, concat_axis=2, tiled=True)]
    another operation x3 -> x0, local copies, waits for them, and re-layouts: 14.1 us -> none  [the longest x1 7.28 us: shards(): spectra = jnp.stack([final_real, final_imag], axis=1).astype(jnp.bfloat16)]
    convert_element_type x0 -> x1, other arithmetic: none -> 11.9 us  [shards(): samples.reshape(local_inputs, local_spec + TAPS - 1, FFT_LEN)]
  transfers between devices with their start and end apart: 1 -> 1, of which waited for: 1 -> 1; matrix products, arithmetic and copies ran while one was open for 0% -> 2% of each run, Pallas kernels for 0% -> 0%
where the time goes in v1:
time: 463 us; the launch traced here: 459 us
  other arithmetic  156 us (34%)
  matrix products  130 us (28%)
  blocking collectives  106 us (23%)
  local copies, waits for them, and re-layouts  60.1 us (13%)
  waiting for transfers between devices  5.01 us (1%)
    dot_general x1, matrix products, shards(): jnp.einsum('rk,kn->nr', rows, table, precision=lax.Precision.HIGH, prefer...  113 us
    all_to_all x1, blocking collectives, shards(): got = lax.all_to_all(spec, ('wide', 'narrow'), 0, 0, tiled=True)  106 us
    add x1, other arithmetic, shards(): filtered + weights_taps[tap_index][None, None, :] * blocks[:, tap_index:t...  99.6 us
    add x1, local copies, waits for them, and re-layouts, shards(): filtered + weights_taps[tap_index][None, None, :] * blocks[:, tap_index:t...  29.3 us
    concatenate x1, other arithmetic, shards(): samples = jnp.concatenate([voltages, after_rows], axis=1)  23.7 us
    dot_general x1, matrix products, shards(): jnp.einsum('csik,cjk->csij', lhs, both, preferred_element_type=jnp.float32)  17.1 us
    convert_element_type x1, other arithmetic, shards(): samples.reshape(local_inputs, local_spec + TAPS - 1, FFT_LEN)  11.9 us
    unnamed x11, local copies, waits for them, and re-layouts  10.6 us
  transfers between devices with their start and end apart: 1, of which 1 were waited for; matrix products, arithmetic and copies ran while one was open for 2% of the time, Pallas kernels for 0%

profile of v1, /device:TPU:1, one launch (start us, length us, event | category | flops | bytes accessed | tf_op | source)
XLA Modules:
  0.0 458.9 jit_solution(10424330434166514943)
XLA Ops:
  0.0 0.0 copy-start.2
  0.0 1.1 slice.122
  1.1 1.3 collective-permute-start
  2.4 0.6 fusion.39
  3.1 1.0 fusion.68
  4.1 0.6 fusion.70
  4.7 0.0 slice-start
  4.8 0.0 slice-start.1
  4.8 7.8 %subtract_multiply_fusion = (f32[32,64,1024]{2,1,0:T(8,128)}, f32[32,64,1024]{2,1,0:T(8,128)}) fusion(f32[64,1024]{1,0:T(8,128)S(1)} %get-tuple-element.30, f32[32,1024]{1,0:T(8,128)S(1)} %get-tuple-element.28, f32[64,1024]{1,0:T(8,128)S(1)} %get-tuple-element.29, f32[32,1024]{1,0:T(8,128)S(1)} %get-tuple-element.27), kind=kLoop, calls=%fused_computation.45 | loop fusion | flops 16777216 | bytes 17563648 | tf_op jit(solution)/shard_map/mul | solution.py:40
  12.6 5.0 %collective-permute-done = bf16[8,30720]{1,0:T(8,128)(2,1)S(1)} collective-permute-done((bf16[8,30720]{1,0:T(8,128)(2,1)S(1)}, bf16[8,30720]{1,0:T(8,128)(2,1)S(1)}, u32[]{:S(2)}, u32[]{:S(2)}) %collective-permute-start) | collective-permute-done | bytes 491552 | tf_op jit(solution)/shard_map/ppermute | solution.py:16
  17.6 0.0 copy-done.2
  17.6 0.1 broadcast_select_fusion
  17.6 0.0 slice-done
  17.6 0.0 slice-done.1
  17.6 23.7 %pad_maximum_fusion.1 = bf16[8,555008]{1,0:T(8,128)(2,1)} fusion(bf16[8,30720]{1,0:T(8,128)(2,1)S(1)} %broadcast_select_fusion, bf16[8,524288]{1,0:T(8,128)(2,1)S(1)} %bitcast.42), kind=kLoop, calls=%fused_computation.39 | loop fusion | flops 17760256 | bytes 17760256 | tf_op jit(solution)/shard_map/concatenate | solution.py:52
  41.3 11.9 %convert.1 = f32[8,271,2048]{2,0,1:T(8,128)} convert(bf16[8,271,2048]{2,0,1:T(8,128)(2,1)} %bitcast.37) | non-fusion elementwise | flops 4440064 | bytes 26640384 | tf_op jit(solution)/shard_map/convert_element_type | solution.py:53
  53.2 99.6 %fusion = f32[8,256,2048]{2,0,1:T(8,128)} fusion(f32[8,271,2048]{2,0,1:T(8,128)} %convert.1, f32[2048]{0:T(1024)S(1)} %get-tuple-element.12, f32[2048]{0:T(1024)S(1)} %get-tuple-element.13, f32[2048]{0:T(1024)S(1)} %get-tuple-element.14, f32[2048]{0:T(1024)S(1)} %get-tuple-element.15, f32[2048]{0:T(1024)S(1)} %get-tuple-element.16, ...), kind=kLoop, calls=%fused_computation.1 | loop fusion | flops 130023424 | bytes 285343744 | tf_op jit(solution)/shard_map/add | solution.py:57
  152.9 29.3 %copy.10 = f32[8,256,2048]{2,1,0:T(8,128)} copy(f32[8,256,2048]{2,0,1:T(8,128)} %fusion) | data formatting | bytes 33554432 | tf_op jit(solution)/shard_map/add | solution.py:57
  182.2 113.2 %fusion.25 = bf16[2048,2048]{1,0:T(8,128)(2,1)} fusion(f32[2048,2048]{1,0:T(8,128)} %bitcast.40, f32[2048,1024]{1,0:T(8,128)} %bitcast.44, f32[2048,1024]{1,0:T(8,128)} %bitcast.43), kind=kOutput, calls=%fused_computation.46 | convolution fusion | flops 51547996160 | bytes 41943040 | tf_op jit(solution)/shard_map/rk,kn->nr/dot_general | solution.py:63
  295.4 10.3 %copy.15 = bf16[256,8,8,256]{3,2,1,0:T(8,128)(2,1)} copy(bf16[256,8,8,256]{3,1,2,0:T(8,128)(2,1)} %bitcast.45) | data formatting | bytes 16777216
  305.7 7.4 %copy_bitcast_fusion = bf16[1024,2,8,256]{3,2,1,0:T(8,128)(2,1)} fusion(bf16[2,1024,8,256]{3,2,1,0:T(8,128)(2,1)} %bitcast.38), kind=kLoop, calls=%fused_computation.43 | loop fusion | bytes 16777216 | tf_op jit(solution)/shard_map/transpose | solution.py:66
  313.1 106.1 %all_to_all.5 = bf16[1024,2,8,256]{3,2,1,0:T(8,128)(2,1)} all-to-all(bf16[1024,2,8,256]{3,2,1,0:T(8,128)(2,1)} %copy_bitcast_fusion), channel_id=1, replica_groups=mesh['wide'=64,'narrow'=2] {'wide','narrow'}, dimensions={0} | all-to-all | bytes 16777216 | tf_op jit(solution)/shard_map/all_to_all | solution.py:67
  419.2 7.6 %copy.12 = bf16[64,2,8,2,8,256]{5,4,1,0,2,3:T(8,128)(2,1)} copy(bf16[64,2,8,2,8,256]{5,4,3,2,1,0:T(8,128)(2,1)} %bitcast.39) | data formatting | bytes 16777216 | tf_op jit(solution)/shard_map/reshape | solution.py:71
  426.8 2.5 fusion.73
  429.3 4.0 slice_bitcast_fusion.1
  433.3 0.0 copy-start
  433.3 0.0 copy-start.1
  433.3 8.0 %fusion.28 = (bf16[8,1,512,1024]{3,2,0,1:T(8,128)(2,1)}, bf16[8,1,512,1024]{3,2,0,1:T(8,128)(2,1)}) fusion(bf16[8,512,512]{2,1,0:T(8,128)(2,1)S(1)} %get-tuple-element.6, bf16[8,512,512]{2,1,0:T(8,128)(2,1)S(1)} %get-tuple-element.5, bf16[8,512,512]{2,1,0:T(8,128)(2,1)S(1)} %fusion.73), kind=kLoop, calls=%fused_computation.47 | loop fusion | flops 33554432 | bytes 29360128 | tf_op jit(solution)/shard_map/stack | solution.py:80
  441.2 0.0 copy-done
  441.2 0.2 copy-done.1
  441.5 17.1 %fusion.21 = f32[8,2,512,512]{3,2,1,0:T(8,128)} fusion(bf16[8,512,512]{2,1,0:T(8,128)(2,1)} %copy-done.1, bf16[8,512,512]{2,1,0:T(8,128)(2,1)} %copy-done, bf16[8,1,512,1024]{3,2,0,1:T(8,128)(2,1)} %get-tuple-element.8, bf16[8,1,512,1024]{3,2,0,1:T(8,128)(2,1)} %get-tuple-element.7), kind=kOutput, calls=%fused_computation.38 | convolution fusion | flops 8619294720 | bytes 41943040 | tf_op jit(solution)/shard_map/csik,cjk->csij/dot_general | solution.py:81
  (4 shorter events, 0.0 us)
Async XLA Ops:
  0.0 17.6 %copy-start.2 = (bf16[8,30720]{1,0:T(8,128)(2,1)S(1)}, bf16[8,30720]{1,0:T(8,128)(2,1)}, u32[]{:S(2)}) copy-start(bf16[8,30720]{1,0:T(8,128)(2,1)} %param.3) | copy-start | bytes 1474564
  1.1 16.4 %collective-permute-start = (bf16[8,30720]{1,0:T(8,128)(2,1)S(1)}, bf16[8,30720]{1,0:T(8,128)(2,1)S(1)}, u32[]{:S(2)}, u32[]{:S(2)}) collective-permute-start(bf16[8,30720]{1,0:T(8,128)(2,1)S(1)} %slice.122), channel_id=1, source_target_pairs={{1,0},{3,2},{5,4},{7,6},{9,8},{11,10},{13,12},{15,14},{17,16},{19,... | collective-permute-start | bytes 1474568 | tf_op jit(solution)/shard_map/ppermute | solution.py:16
  4.7 12.9 %slice-start = ((s8[8388608]{0:T(1024)(128)(4,1)}), s8[4194304]{0:T(1024)(128)(4,1)S(1)}, s32[]{:S(2)}) async-start(s8[8388608]{0:T(1024)(128)(4,1)} %bitcast.41), calls=%async_computation.1 | async-start | bytes 8388608
  4.8 12.9 %slice-start.1 = ((s8[8388608]{0:T(1024)(128)(4,1)}), s8[4194304]{0:T(1024)(128)(4,1)S(1)}, s32[]{:S(2)}) async-start(s8[8388608]{0:T(1024)(128)(4,1)} %bitcast.41), calls=%async_computation.2 | async-start | bytes 8388608
  433.3 8.0 %copy-start = (bf16[8,512,512]{2,1,0:T(8,128)(2,1)}, bf16[8,512,512]{2,1,0:T(8,128)(2,1)S(1)}, u32[]{:S(2)}) copy-start(bf16[8,512,512]{2,1,0:T(8,128)(2,1)S(1)} %get-tuple-element.5) | copy-start | bytes 12582916
  433.3 8.2 %copy-start.1 = (bf16[8,512,512]{2,1,0:T(8,128)(2,1)}, bf16[8,512,512]{2,1,0:T(8,128)(2,1)S(1)}, u32[]{:S(2)}) copy-start(bf16[8,512,512]{2,1,0:T(8,128)(2,1)S(1)} %get-tuple-element.6) | copy-start | bytes 12582916

commit v2 on v1

v2 whole, which is shorter than its diff:
```python
import functools
import math

import jax
import jax.numpy as jnp
from jax import lax
from jax.experimental import pallas as pl
from jax.experimental.pallas import tpu as pltpu
from jax.sharding import PartitionSpec as P

FFT_LEN = 2048
CHANNELS = 1024
TAPS = 16
PHASES = 8
SUB_LEN = FFT_LEN // PHASES
CHUNK = 32


def from_behind(x, axis, by):
    size = lax.axis_size(axis)
    pairs = [(i, i + by) for i in range(size) if 0 <= i + by < size]
    return lax.ppermute(x, axis, pairs)


def pfb_window(block_len, tap_count):
    length_all = tap_count * block_len
    sample_pos = jnp.arange(length_all, dtype=jnp.float32)
    centred = (sample_pos + 0.5 - length_all / 2.0) / block_len
    taper = 0.5 - 0.5 * jnp.cos(2.0 * jnp.pi * (sample_pos + 0.5) / length_all)
    return jnp.sinc(centred) * taper


def phase_matrices(salt):
    k1 = jnp.arange(SUB_LEN, dtype=jnp.int32)[None, :, None]
    c1 = jnp.arange(CHANNELS // PHASES, dtype=jnp.int32)[None, None, :] + salt
    c2 = jnp.arange(PHASES, dtype=jnp.int32)[:, None, None]
    turns = (k1 * (PHASES * c1 + c2)) % FFT_LEN
    angles = (2.0 * jnp.pi / FFT_LEN) * turns.astype(jnp.float32)
    scaling = 1.0 / math.sqrt(FFT_LEN)
    cos_t = jnp.cos(angles) * scaling
    sin_t = jnp.sin(angles) * scaling
    top = jnp.concatenate([cos_t, -sin_t], axis=-1)
    bottom = jnp.concatenate([sin_t, cos_t], axis=-1)
    full = jnp.concatenate([top, bottom], axis=1)
    high = full.astype(jnp.bfloat16)
    low = (full - high.astype(jnp.float32)).astype(jnp.bfloat16)
    return high, low


def split_parts(value):
    high = value.astype(jnp.bfloat16)
    low = (value - high.astype(jnp.float32)).astype(jnp.bfloat16)
    return high, low


def spectra_kernel(xa_ref, xh_ref, wb_ref, bh_ref, bl_ref, out_ref,
                   xf_ref, f_ref, uh_ref, ul_ref):
    step = pl.program_id(0)
    last = pl.num_programs(0) - 1
    halo = TAPS - 1

    def load_block(q_local, _):
        q = step * CHUNK + q_local
        start = pl.multiple_of(q * FFT_LEN, FFT_LEN)
        xf_ref[q_local] = xa_ref[:, pl.ds(start, FFT_LEN)].astype(jnp.float32)
        return 0

    lax.fori_loop(0, CHUNK, load_block, 0)

    @pl.when(step < last)
    def _():
        def body(j, _):
            q = (step + 1) * CHUNK + j
            start = pl.multiple_of(q * FFT_LEN, FFT_LEN)
            xf_ref[CHUNK + j] = xa_ref[:, pl.ds(start, FFT_LEN)].astype(jnp.float32)
            return 0
        lax.fori_loop(0, halo, body, 0)

    @pl.when(step == last)
    def _():
        def body(j, _):
            start = pl.multiple_of(j * FFT_LEN, FFT_LEN)
            xf_ref[CHUNK + j] = xh_ref[:, pl.ds(start, FFT_LEN)].astype(jnp.float32)
            return 0
        lax.fori_loop(0, halo, body, 0)

    lane_w = 256
    for lane_at in range(FFT_LEN // lane_w):
        lanes = slice(lane_at * lane_w, (lane_at + 1) * lane_w)
        taps = [wb_ref[p, :, lanes] for p in range(TAPS)]

        def filt(ml, _):
            acc = taps[0] * xf_ref[ml, :, lanes]
            for p in range(1, TAPS):
                acc = acc + taps[p] * xf_ref[ml + p, :, lanes]
            row = pl.multiple_of(ml * 8, 8)
            f_ref[pl.ds(row, 8), lanes] = acc
            return 0

        lax.fori_loop(0, CHUNK, filt, 0)

    half = 1.0 / math.sqrt(2.0)
    rows_per = 16

    def butterflies(g, _):
        row = pl.multiple_of(g * rows_per, rows_per)
        rs = pl.ds(row, rows_per)
        a = [f_ref[rs, n * SUB_LEN:(n + 1) * SUB_LEN] for n in range(PHASES)]
        s04 = a[0] + a[4]
        d04 = a[0] - a[4]
        s26 = a[2] + a[6]
        d26 = a[2] - a[6]
        s15 = a[1] + a[5]
        d15 = a[1] - a[5]
        s37 = a[3] + a[7]
        d37 = a[3] - a[7]
        e0 = s04 + s26
        e2 = s04 - s26
        o0 = s15 + s37
        o2 = s15 - s37
        p = half * (d15 - d37)
        q = half * (d15 + d37)
        outs = [
            (e0 + o0, None),
            (d04 + p, -d26 - q),
            (e2, -o2),
            (d04 - p, d26 - q),
            (e0 - o0, None),
            (d04 - p, -d26 + q),
            (e2, o2),
            (d04 + p, d26 + q),
        ]
        for c2, (re, im) in enumerate(outs):
            hi, lo = split_parts(re)
            uh_ref[c2, rs, 0:SUB_LEN] = hi
            ul_ref[c2, rs, 0:SUB_LEN] = lo
            if im is not None:
                hi, lo = split_parts(im)
                uh_ref[c2, rs, SUB_LEN:2 * SUB_LEN] = hi
                ul_ref[c2, rs, SUB_LEN:2 * SUB_LEN] = lo
        return 0

    lax.fori_loop(0, (CHUNK * 8) // rows_per, butterflies, 0)

    for c2 in range(PHASES):
        depth = SUB_LEN if c2 in (0, PHASES // 2) else 2 * SUB_LEN
        lh = uh_ref[c2, :, 0:depth]
        ll = ul_ref[c2, :, 0:depth]
        bh = bh_ref[c2, 0:depth, :]
        bl = bl_ref[c2, 0:depth, :]
        acc = jnp.dot(lh, bh, preferred_element_type=jnp.float32)
        acc = acc + jnp.dot(ll, bh, preferred_element_type=jnp.float32)
        acc = acc + jnp.dot(lh, bl, preferred_element_type=jnp.float32)
        out_ref[0, c2] = acc.astype(jnp.bfloat16)


def pfb_spectra(xa, xh, wb, bh, bl):
    n_in, span = xa.shape
    n_spec = span // FFT_LEN
    steps = n_spec // CHUNK
    rows = CHUNK * n_in
    flops = 2 * steps * rows * 3 * SUB_LEN * 2 * SUB_LEN * 7 + 2 * n_in * n_spec * FFT_LEN * TAPS
    bytes_accessed = xa.size * 2 + xh.size * 2 + steps * PHASES * rows * 2 * SUB_LEN * 2
    return pl.pallas_call(
        spectra_kernel,
        out_shape=jax.ShapeDtypeStruct((steps, PHASES, rows, CHANNELS // PHASES * 2), jnp.bfloat16),
        grid=(steps,),
        in_specs=[
            pl.BlockSpec((n_in, span), lambda s: (0, 0), pipeline_mode=pl.Buffered(1)),
            pl.BlockSpec(xh.shape, lambda s: (0, 0), pipeline_mode=pl.Buffered(1)),
            pl.BlockSpec(wb.shape, lambda s: (0, 0, 0), pipeline_mode=pl.Buffered(1)),
            pl.BlockSpec(bh.shape, lambda s: (0, 0, 0), pipeline_mode=pl.Buffered(1)),
            pl.BlockSpec(bl.shape, lambda s: (0, 0, 0), pipeline_mode=pl.Buffered(1)),
        ],
        out_specs=pl.BlockSpec((1, PHASES, rows, CHANNELS // PHASES * 2), lambda s: (s, 0, 0, 0)),
        scratch_shapes=[
            pltpu.VMEM((CHUNK + TAPS - 1, n_in, FFT_LEN), jnp.float32),
            pltpu.VMEM((rows, FFT_LEN), jnp.float32),
            pltpu.VMEM((PHASES, rows, 2 * SUB_LEN), jnp.bfloat16),
            pltpu.VMEM((PHASES, rows, 2 * SUB_LEN), jnp.bfloat16),
        ],
        compiler_params=pltpu.CompilerParams(
            dimension_semantics=("arbitrary",), vmem_limit_bytes=60 * 1024 * 1024
        ),
        cost_estimate=pl.CostEstimate(flops=flops, transcendentals=0, bytes_accessed=bytes_accessed),
    )(xa, xh, wb, bh, bl)


def shards(voltages, following):
    local_inputs, local_span = voltages.shape
    local_spec = local_span // FFT_LEN
    halo_len = (TAPS - 1) * FFT_LEN
    leading = voltages[:, :halo_len]
    shifted = from_behind(leading, "narrow", -1)
    is_final = lax.axis_index("narrow") == lax.axis_size("narrow") - 1
    after_rows = jnp.where(is_final, following, shifted)
    weights_taps = pfb_window(FFT_LEN, TAPS).reshape(TAPS, 1, FFT_LEN)
    wb = jnp.broadcast_to(weights_taps, (TAPS, local_inputs, FFT_LEN))
    salt = lax.optimization_barrier(jnp.zeros((), jnp.int32))
    bh, bl = phase_matrices(salt)
    out = pfb_spectra(voltages, after_rows, wb, bh, bl)
    steps = local_spec // CHUNK
    c1_len = CHANNELS // PHASES
    out = out.reshape(steps, PHASES, CHUNK, local_inputs, 2, c1_len)
    spec = jnp.transpose(out, (5, 1, 4, 3, 0, 2)).reshape(CHANNELS, 2, local_inputs, local_spec)
    got = lax.all_to_all(spec, ("wide", "narrow"), 0, 0, tiled=True)
    n_wide = lax.axis_size("wide")
    n_narrow = lax.axis_size("narrow")
    chan_dev = CHANNELS // (n_wide * n_narrow)
    got = got.reshape(n_wide, n_narrow, chan_dev, 2, local_inputs, local_spec)
    got = jnp.transpose(got, (2, 3, 0, 4, 1, 5))
    all_inputs = n_wide * local_inputs
    time_len = n_narrow * local_spec
    got = got.reshape(chan_dev, 2, all_inputs, time_len)
    re = got[:, 0]
    im = got[:, 1]
    both = jnp.concatenate([re, im], axis=-1)
    turned = jnp.concatenate([im, -re], axis=-1)
    lhs = jnp.stack([both, turned], axis=1)
    vis = jnp.einsum("csik,cjk->csij", lhs, both, preferred_element_type=jnp.float32)
    return vis * (1.0 / time_len)


def solution(mesh):
    in_specs = (P("wide", "narrow"), P("wide", None))
    out_specs = P(("wide", "narrow"), None, None, None)
    return jax.shard_map(shards, mesh=mesh, in_specs=in_specs, out_specs=out_specs, check_vma=False)
```

time: 463 us -> 330 us (0.71)
  other arithmetic: 156 us -> 20.7 us
  matrix products: 130 us -> 17.1 us
  Pallas kernels: 0 us -> 65.7 us
  local copies, waits for them, and re-layouts: 60.1 us -> 109 us
    dot_general x1 -> x0, matrix products: 113 us -> none  [shards(): jnp.einsum('rk,kn->nr', rows, table, precision=lax.Precision.HIGH, prefer...]
    add x2 -> x1, other arithmetic: 99.7 us -> 0.01 us  [phase_matrices(): turns = k1 * (PHASES * c1 + c2) % FFT_LEN]
    reshape x1 -> x2, local copies, waits for them, and re-layouts: 7.62 us -> 95.8 us  [the longest x1 56.3 us: shards(): out = out.reshape(steps, PHASES, CHUNK, local_inputs, 2, c1_len)]
    pallas_call x0 -> x1, Pallas kernels: none -> 65.7 us  [pfb_spectra(): pl.pallas_call(spectra_kernel, out_shape=jax.ShapeDtypeStruct((steps, PHA...]
    add x1 -> x0, local copies, waits for them, and re-layouts: 29.3 us -> none  [shards(): filtered + weights_taps[tap_index][None, None, :] * blocks[:, tap_index:t...]
    concatenate x1 -> x0, other arithmetic: 23.7 us -> none  [shards(): samples = jnp.concatenate([voltages, after_rows], axis=1)]
    convert_element_type x1 -> x2, other arithmetic: 11.9 us -> 3.38 us  [the longest x1 1.79 us: phase_matrices(): low = (full - high.astype(jnp.float32)).astype(jnp.bfloat16)]
    unnamed x11 -> x6, local copies, waits for them, and re-layouts: 10.6 us -> 2.32 us
  transfers between devices with their start and end apart: 1 -> 1, of which waited for: 1 -> 1; matrix products, arithmetic and copies ran while one was open for 2% -> 3% of each run, Pallas kernels for 0% -> 0%
where the time goes in v2:
time: 330 us; the launch traced here: 327 us
  local copies, waits for them, and re-layouts  109 us (33%)
  blocking collectives  106 us (32%)
  Pallas kernels  65.7 us (20%)
  other arithmetic  20.7 us (6%)
  matrix products  17.1 us (5%)
  waiting for transfers between devices  7.25 us (2%)
    all_to_all x1, blocking collectives, shards(): got = lax.all_to_all(spec, ('wide', 'narrow'), 0, 0, tiled=True)  106 us
    pallas_call x1, Pallas kernels, pfb_spectra(): pl.pallas_call(spectra_kernel, out_shape=jax.ShapeDtypeStruct((steps, PHA...  65.7 us
    reshape x1, local copies, waits for them, and re-layouts, shards(): out = out.reshape(steps, PHASES, CHUNK, local_inputs, 2, c1_len)  56.3 us
    reshape x1, local copies, waits for them, and re-layouts, shards(): jnp.transpose(out, (5, 1, 4, 3, 0, 2))  39.4 us
    dot_general x1, matrix products, shards(): jnp.einsum('csik,cjk->csij', lhs, both, preferred_element_type=jnp.float32)  17.1 us
    another operation x1, other arithmetic, shards(): lhs = jnp.stack([both, turned], axis=1)  7.98 us
    transpose x1, local copies, waits for them, and re-layouts, shards(): got = jnp.transpose(got, (2, 3, 0, 4, 1, 5))  7.62 us
    ppermute x1, waiting for transfers between devices, from_behind(): return lax.ppermute(x, axis, pairs)  7.25 us
  transfers between devices with their start and end apart: 1, of which 1 were waited for; matrix products, arithmetic and copies ran while one was open for 3% of the time, Pallas kernels for 0%

profile of v2, /device:TPU:1, one launch (start us, length us, event | category | flops | bytes accessed | tf_op | source)
XLA Modules:
  0.0 327.3 jit_solution(5240587703266680018)
XLA Ops:
  0.0 1.8 slice.9
  1.8 1.3 collective-permute-start
  3.2 4.2 %fusion.14 = (f32[8,256,128]{2,1,0:T(8,128)S(1)}, f32[8,256,128]{2,1,0:T(8,128)S(1)}, f32[8,256,128]{2,1,0:T(8,128)S(1)}) fusion(s32[8,128]{1,0:T(8,128)S(1)} %iota_add_fusion), kind=kLoop, calls=%fused_computation.25 | loop fusion | flops 4456448 | bytes 3149824 | tf_op jit(solution)/shard_map/neg | solution.py:42
  7.3 1.6 fusion.7.bh_ref
  8.9 1.8 subtract_convert_fusion.bl_ref
  10.7 0.6 fusion.19
  11.3 7.2 %collective-permute-done = bf16[8,30720]{1,0:T(8,128)(2,1)} collective-permute-done((bf16[8,30720]{1,0:T(8,128)(2,1)}, bf16[8,30720]{1,0:T(8,128)(2,1)}, u32[]{:S(2)}, u32[]{:S(2)}) %collective-permute-start) | collective-permute-done | bytes 491552 | tf_op jit(solution)/shard_map/ppermute | solution.py:22
  18.6 1.9 broadcast_select_fusion.xh_ref
  20.5 1.1 broadcast_in_dim.7.wb_ref
  21.6 65.7 %shard_map.28 = bf16[8,8,256,256]{3,2,1,0:T(8,128)(2,1)} custom-call(bf16[8,524288]{1,0:T(8,128)(2,1)} %xa_ref.1, bf16[8,30720]{1,0:T(8,128)(2,1)} %broadcast_select_fusion.xh_ref, f32[16,8,2048]{2,1,0:T(8,128)} %broadcast_in_dim.7.wb_ref, bf16[8,512,256]{2,1,0:T(8,128)(2,1)} %fusion.7.bh_ref, bf16[8,512,256]{2,1,0:T(8,128)(2,1)} %subtract_convert_fusion.bl_ref), custom_call_target="tpu_custom_call" | custom-call | flops 11408506880 | bytes 25657344 | tf_op jit(solution)/shard_map/pallas_call | solution.py:164
  87.2 56.3 %copy.4 = bf16[8,8,32,8,2,128]{2,0,3,4,1,5:T(8,128)(2,1)} copy(bf16[8,8,32,8,2,128]{5,3,4,2,1,0:T(8,128)(2,1)} %bitcast.27) | data formatting | bytes 16777216 | tf_op jit(solution)/shard_map/reshape | solution.py:204
  143.6 39.4 %reshape.91 = bf16[1024,2,8,256]{3,2,1,0:T(8,128)(2,1)} reshape(bf16[128,8,2,8,8,32]{5,4,3,2,1,0:T(8,128)(2,1)} %bitcast.23) | data formatting | bytes 16777216 | tf_op jit(solution)/shard_map/reshape | solution.py:205
  183.0 106.0 %all_to_all.5 = bf16[1024,2,8,256]{3,2,1,0:T(8,128)(2,1)} all-to-all(bf16[1024,2,8,256]{3,2,1,0:T(8,128)(2,1)} %reshape.91), channel_id=1, replica_groups=mesh['wide'=64,'narrow'=2] {'wide','narrow'}, dimensions={0} | all-to-all | bytes 16777216 | tf_op jit(solution)/shard_map/all_to_all | solution.py:206
  289.1 7.6 %copy.5 = bf16[8,2,64,8,2,256]{5,3,4,2,0,1:T(8,128)(2,1)} copy(bf16[8,2,64,8,2,256]{5,3,1,0,4,2:T(8,128)(2,1)} %bitcast.26) | data formatting | bytes 16777216 | tf_op jit(solution)/shard_map/transpose | solution.py:211
  296.7 0.0 copy-start
  296.7 2.6 fusion.29
  299.3 2.0 copy-done
  301.3 0.6 slice_bitcast_fusion.1
  301.9 0.0 copy-start.1
  301.9 0.0 copy-start.2
  301.9 8.0 %fusion.6 = (bf16[8,1,512,1024]{3,2,0,1:T(8,128)(2,1)}, bf16[8,1,512,1024]{3,2,0,1:T(8,128)(2,1)}) fusion(bf16[8,512,512]{2,1,0:T(8,128)(2,1)S(1)} %get-tuple-element.6, bf16[8,512,512]{2,1,0:T(8,128)(2,1)S(1)} %get-tuple-element.5, bf16[8,512,512]{2,1,0:T(8,128)(2,1)S(1)} %fusion.29), kind=kLoop, calls=%fused_computation.7 | loop fusion | flops 33554432 | bytes 29360128 | tf_op jit(solution)/shard_map/stack | solution.py:219
  309.9 0.0 copy-done.1
  309.9 0.3 copy-done.2
  310.2 17.1 %fusion.2 = f32[8,2,512,512]{3,2,1,0:T(8,128)} fusion(bf16[8,512,512]{2,1,0:T(8,128)(2,1)} %copy-done.2, bf16[8,512,512]{2,1,0:T(8,128)(2,1)} %copy-done.1, bf16[8,1,512,1024]{3,2,0,1:T(8,128)(2,1)} %get-tuple-element.8, bf16[8,1,512,1024]{3,2,0,1:T(8,128)(2,1)} %get-tuple-element.7), kind=kOutput, calls=%fused_computation.3 | convolution fusion | flops 8619294720 | bytes 41943040 | tf_op jit(solution)/shard_map/csik,cjk->csij/dot_general | solution.py:220
  (2 shorter events, 0.0 us)
Async XLA Ops:
  1.8 16.7 %collective-permute-start = (bf16[8,30720]{1,0:T(8,128)(2,1)}, bf16[8,30720]{1,0:T(8,128)(2,1)}, u32[]{:S(2)}, u32[]{:S(2)}) collective-permute-start(bf16[8,30720]{1,0:T(8,128)(2,1)} %slice.9), channel_id=1, source_target_pairs={{1,0},{3,2},{5,4},{7,6},{9,8},{11,10},{13,12},{15,14},{17,16},{19,... | collective-permute-start | bytes 1474568 | tf_op jit(solution)/shard_map/ppermute | solution.py:22
  296.7 4.6 %copy-start = (bf16[8,2,64,8,2,256]{5,3,4,2,0,1:T(8,128)(2,1)S(1)}, bf16[8,2,64,8,2,256]{5,3,4,2,0,1:T(8,128)(2,1)}, u32[]{:S(2)}) copy-start(bf16[8,2,64,8,2,256]{5,3,4,2,0,1:T(8,128)(2,1)} %copy.5) | copy-start | bytes 25165828
  301.9 8.0 %copy-start.1 = (bf16[8,512,512]{2,1,0:T(8,128)(2,1)}, bf16[8,512,512]{2,1,0:T(8,128)(2,1)S(1)}, u32[]{:S(2)}) copy-start(bf16[8,512,512]{2,1,0:T(8,128)(2,1)S(1)} %get-tuple-element.5) | copy-start | bytes 12582916
  301.9 8.3 %copy-start.2 = (bf16[8,512,512]{2,1,0:T(8,128)(2,1)}, bf16[8,512,512]{2,1,0:T(8,128)(2,1)S(1)}, u32[]{:S(2)}) copy-start(bf16[8,512,512]{2,1,0:T(8,128)(2,1)S(1)} %get-tuple-element.6) | copy-start | bytes 12582916

commit v3 on v2

v3 whole, which is shorter than its diff:
```python
import functools
import math

import jax
import jax.numpy as jnp
from jax import lax
from jax.experimental import pallas as pl
from jax.experimental.pallas import tpu as pltpu
from jax.sharding import PartitionSpec as P

FFT_LEN = 2048
CHANNELS = 1024
TAPS = 16
PHASES = 8
SUB_LEN = FFT_LEN // PHASES
CHUNK = 128


def from_behind(x, axis, by):
    size = lax.axis_size(axis)
    pairs = [(i, i + by) for i in range(size) if 0 <= i + by < size]
    return lax.ppermute(x, axis, pairs)


def pfb_window(block_len, tap_count):
    length_all = tap_count * block_len
    sample_pos = jnp.arange(length_all, dtype=jnp.float32)
    centred = (sample_pos + 0.5 - length_all / 2.0) / block_len
    taper = 0.5 - 0.5 * jnp.cos(2.0 * jnp.pi * (sample_pos + 0.5) / length_all)
    return jnp.sinc(centred) * taper


def phase_matrices(salt):
    k1 = jnp.arange(SUB_LEN, dtype=jnp.int32)[None, None, :]
    c1 = jnp.arange(CHANNELS // PHASES, dtype=jnp.int32)[None, :, None] + salt
    c2 = jnp.arange(PHASES, dtype=jnp.int32)[:, None, None]
    turns = (k1 * (PHASES * c1 + c2)) % FFT_LEN
    angles = (2.0 * jnp.pi / FFT_LEN) * turns.astype(jnp.float32)
    scaling = 1.0 / math.sqrt(FFT_LEN)
    cos_t = jnp.cos(angles) * scaling
    sin_t = jnp.sin(angles) * scaling
    real_row = jnp.concatenate([cos_t, sin_t], axis=-1)
    imag_row = jnp.concatenate([-sin_t, cos_t], axis=-1)
    full = jnp.concatenate([real_row, imag_row], axis=1)
    high = full.astype(jnp.bfloat16)
    low = (full - high.astype(jnp.float32)).astype(jnp.bfloat16)
    return high, low


def split_parts(value):
    high = value.astype(jnp.bfloat16)
    low = (value - high.astype(jnp.float32)).astype(jnp.bfloat16)
    return high, low


def nearest_bf16(value):
    scaled = value * 65537.0
    return (scaled - (scaled - value)).astype(jnp.bfloat16)


def spectra_kernel(xa_ref, xh_ref, wb_ref, bh_ref, bl_ref, out_ref,
                   xf_ref, f_ref, uh_ref, ul_ref):
    step = pl.program_id(0)
    last = pl.num_programs(0) - 1
    halo = TAPS - 1
    n_in = xa_ref.shape[0]

    def load_block(q_local, _):
        q = step * CHUNK + q_local
        start = pl.multiple_of(q * FFT_LEN, FFT_LEN)
        xf_ref[q_local] = xa_ref[:, pl.ds(start, FFT_LEN)].astype(jnp.float32)
        return 0

    lax.fori_loop(0, CHUNK, load_block, 0)

    @pl.when(step < last)
    def _():
        def body(j, _):
            q = (step + 1) * CHUNK + j
            start = pl.multiple_of(q * FFT_LEN, FFT_LEN)
            xf_ref[CHUNK + j] = xa_ref[:, pl.ds(start, FFT_LEN)].astype(jnp.float32)
            return 0
        lax.fori_loop(0, halo, body, 0)

    @pl.when(step == last)
    def _():
        def body(j, _):
            start = pl.multiple_of(j * FFT_LEN, FFT_LEN)
            xf_ref[CHUNK + j] = xh_ref[:, pl.ds(start, FFT_LEN)].astype(jnp.float32)
            return 0
        lax.fori_loop(0, halo, body, 0)

    lane_w = 128
    for lane_at in range(FFT_LEN // lane_w):
        lanes = slice(lane_at * lane_w, (lane_at + 1) * lane_w)
        taps = [wb_ref[p, :, lanes] for p in range(TAPS)]

        def filt(ml, _):
            acc = taps[0] * xf_ref[ml, :, lanes]
            for p in range(1, TAPS):
                acc = acc + taps[p] * xf_ref[ml + p, :, lanes]
            f_ref[lane_at, pl.ds(ml, n_in, stride=CHUNK), :] = acc
            return 0

        lax.fori_loop(0, CHUNK, filt, 0)

    half = 1.0 / math.sqrt(2.0)
    rows_per = 16
    sub_rows = 256

    for sub in range((CHUNK * n_in) // sub_rows):

        def butterflies(g, _):
            row = pl.multiple_of(sub * sub_rows + g * rows_per, rows_per)
            local = pl.multiple_of(g * rows_per, rows_per)
            rs = pl.ds(row, rows_per)
            ls = pl.ds(local, rows_per)
            for h in range(2):
                a = [f_ref[2 * n + h, rs, :] for n in range(PHASES)]
                s04 = a[0] + a[4]
                d04 = a[0] - a[4]
                s26 = a[2] + a[6]
                d26 = a[2] - a[6]
                s15 = a[1] + a[5]
                d15 = a[1] - a[5]
                s37 = a[3] + a[7]
                d37 = a[3] - a[7]
                e0 = s04 + s26
                e2 = s04 - s26
                o0 = s15 + s37
                o2 = s15 - s37
                p = half * (d15 - d37)
                q = half * (d15 + d37)
                outs = [
                    (e0 + o0, None),
                    (d04 + p, -d26 - q),
                    (e2, -o2),
                    (d04 - p, d26 - q),
                    (e0 - o0, None),
                    (d04 - p, -d26 + q),
                    (e2, o2),
                    (d04 + p, d26 + q),
                ]
                re_l = slice(h * 128, (h + 1) * 128)
                im_l = slice(SUB_LEN + h * 128, SUB_LEN + (h + 1) * 128)
                for c2, (re, im) in enumerate(outs):
                    hi, lo = split_parts(re)
                    uh_ref[c2, ls, re_l] = hi
                    ul_ref[c2, ls, re_l] = lo
                    if im is not None:
                        hi, lo = split_parts(im)
                        uh_ref[c2, ls, im_l] = hi
                        ul_ref[c2, ls, im_l] = lo
            return 0

        lax.fori_loop(0, sub_rows // rows_per, butterflies, 0)

        nt = (((1,), (1,)), ((), ()))
        for c2 in range(PHASES):
            depth = SUB_LEN if c2 in (0, PHASES // 2) else 2 * SUB_LEN
            uh = uh_ref[c2, :, 0:depth]
            ul = ul_ref[c2, :, 0:depth]
            bh = bh_ref[c2, :, 0:depth]
            bl = bl_ref[c2, :, 0:depth]
            acc = lax.dot_general(bh, uh, nt, preferred_element_type=jnp.float32)
            acc = acc + lax.dot_general(bh, ul, nt, preferred_element_type=jnp.float32)
            acc = acc + lax.dot_general(bl, uh, nt, preferred_element_type=jnp.float32)
            out_ref[0, c2, :, sub * sub_rows:(sub + 1) * sub_rows] = nearest_bf16(acc)


def pfb_spectra(xa, xh, wb, bh, bl):
    n_in, span = xa.shape
    n_spec = span // FFT_LEN
    steps = n_spec // CHUNK
    rows = CHUNK * n_in
    flops = 2 * steps * rows * 3 * SUB_LEN * 2 * SUB_LEN * 7 + 2 * n_in * n_spec * FFT_LEN * TAPS
    bytes_accessed = xa.size * 2 + xh.size * 2 + steps * PHASES * rows * 2 * SUB_LEN * 2
    return pl.pallas_call(
        spectra_kernel,
        out_shape=jax.ShapeDtypeStruct((steps, PHASES, 2 * CHANNELS // PHASES, rows), jnp.bfloat16),
        grid=(steps,),
        in_specs=[
            pl.BlockSpec((n_in, span), lambda s: (0, 0), pipeline_mode=pl.Buffered(1)),
            pl.BlockSpec(xh.shape, lambda s: (0, 0), pipeline_mode=pl.Buffered(1)),
            pl.BlockSpec(wb.shape, lambda s: (0, 0, 0), pipeline_mode=pl.Buffered(1)),
            pl.BlockSpec(bh.shape, lambda s: (0, 0, 0), pipeline_mode=pl.Buffered(1)),
            pl.BlockSpec(bl.shape, lambda s: (0, 0, 0), pipeline_mode=pl.Buffered(1)),
        ],
        out_specs=pl.BlockSpec((1, PHASES, 2 * CHANNELS // PHASES, rows), lambda s: (s, 0, 0, 0)),
        scratch_shapes=[
            pltpu.VMEM((CHUNK + TAPS - 1, n_in, FFT_LEN), jnp.float32),
            pltpu.VMEM((FFT_LEN // 128, rows, 128), jnp.float32),
            pltpu.VMEM((PHASES, 256, 2 * SUB_LEN), jnp.bfloat16),
            pltpu.VMEM((PHASES, 256, 2 * SUB_LEN), jnp.bfloat16),
        ],
        compiler_params=pltpu.CompilerParams(
            dimension_semantics=("arbitrary",), vmem_limit_bytes=62 * 1024 * 1024
        ),
        cost_estimate=pl.CostEstimate(flops=flops, transcendentals=0, bytes_accessed=bytes_accessed),
    )(xa, xh, wb, bh, bl)


def shards(voltages, following):
    local_inputs, local_span = voltages.shape
    local_spec = local_span // FFT_LEN
    halo_len = (TAPS - 1) * FFT_LEN
    leading = voltages[:, :halo_len]
    shifted = from_behind(leading, "narrow", -1)
    is_final = lax.axis_index("narrow") == lax.axis_size("narrow") - 1
    after_rows = jnp.where(is_final, following, shifted)
    weights_taps = pfb_window(FFT_LEN, TAPS).reshape(TAPS, 1, FFT_LEN)
    wb = jnp.broadcast_to(weights_taps, (TAPS, local_inputs, FFT_LEN))
    salt = lax.optimization_barrier(jnp.zeros((), jnp.int32))
    bh, bl = phase_matrices(salt)
    out = pfb_spectra(voltages, after_rows, wb, bh, bl)
    steps = local_spec // CHUNK
    c1_len = CHANNELS // PHASES
    out = out.reshape(steps, PHASES, 2, c1_len, local_inputs, CHUNK)
    spec = jnp.transpose(out, (3, 1, 2, 0, 4, 5))
    got = lax.all_to_all(spec, ("wide", "narrow"), 0, 0, tiled=True)
    n_wide = lax.axis_size("wide")
    n_narrow = lax.axis_size("narrow")
    got = got.reshape(n_wide, n_narrow, PHASES, 2, steps, local_inputs, CHUNK)
    got = jnp.transpose(got, (2, 0, 5, 3, 1, 4, 6))
    all_inputs = n_wide * local_inputs
    time_len = n_narrow * local_spec
    got = got.reshape(PHASES, all_inputs, 2, time_len)
    both = got.reshape(PHASES, all_inputs, 2 * time_len)
    turned = jnp.concatenate([got[:, :, 1], -got[:, :, 0]], axis=-1)
    lhs = jnp.stack([both, turned], axis=1)
    vis = jnp.einsum("csik,cjk->csij", lhs, both, preferred_element_type=jnp.float32)
    return vis * (1.0 / time_len)


def solution(mesh):
    in_specs = (P("wide", "narrow"), P("wide", None))
    out_specs = P(("wide", "narrow"), None, None, None)
    return jax.shard_map(shards, mesh=mesh, in_specs=in_specs, out_specs=out_specs, check_vma=False)
```

time: 330 us -> 310 us (0.939)
  local copies, waits for them, and re-layouts: 109 us -> 38.9 us
  Pallas kernels: 65.7 us -> 111 us
    reshape x2, local copies, waits for them, and re-layouts: 95.8 us -> 18.3 us  [the longest x1 9.19 us: shards(): out = out.reshape(steps, PHASES, 2, c1_len, local_inputs, CHUNK)]
    pallas_call x1, Pallas kernels: 65.7 us -> 111 us  [pfb_spectra(): pl.pallas_call(spectra_kernel, out_shape=jax.ShapeDtypeStruct((steps, PHA...]
    neg x2 -> x0, other arithmetic: 6.78 us -> none  [the longest x1 4.17 us: phase_matrices(): top = jnp.concatenate([cos_t, -sin_t], axis=-1)]
    unnamed x6 -> x3, local copies, waits for them, and re-layouts: 2.32 us -> 8.77 us
    squeeze x0 -> x1, other arithmetic: none -> 5.72 us  [shards(): turned = jnp.concatenate([got[:, :, 1], -got[:, :, 0]], axis=-1)]
    mul x0 -> x1, other arithmetic: none -> 4.26 us  [phase_matrices(): sin_t = jnp.sin(angles) * scaling]
where the time goes in v3:
time: 310 us; the launch traced here: 309 us
  Pallas kernels  111 us (36%)
  blocking collectives  106 us (34%)
  local copies, waits for them, and re-layouts  38.9 us (13%)
  other arithmetic  23.5 us (8%)
  matrix products  20.4 us (7%)
  waiting for transfers between devices  7.27 us (2%)
    pallas_call x1, Pallas kernels, pfb_spectra(): pl.pallas_call(spectra_kernel, out_shape=jax.ShapeDtypeStruct((steps, PHA...  111 us
    all_to_all x1, blocking collectives, shards(): got = lax.all_to_all(spec, ('wide', 'narrow'), 0, 0, tiled=True)  106 us
    dot_general x1, matrix products, shards(): jnp.einsum('csik,cjk->csij', lhs, both, preferred_element_type=jnp.float32)  20.4 us
    reshape x1, local copies, waits for them, and re-layouts, shards(): out = out.reshape(steps, PHASES, 2, c1_len, local_inputs, CHUNK)  9.19 us
    reshape x1, local copies, waits for them, and re-layouts, shards(): got = got.reshape(n_wide, n_narrow, PHASES, 2, steps, local_inputs, CHUNK)  9.07 us
    transpose x1, local copies, waits for them, and re-layouts, shards(): got = jnp.transpose(got, (2, 0, 5, 3, 1, 4, 6))  8.95 us
    unnamed x3, local copies, waits for them, and re-layouts  8.77 us
    another operation x1, other arithmetic, shards(): lhs = jnp.stack([both, turned], axis=1)  7.78 us
  transfers between devices with their start and end apart: 1, of which 1 were waited for; matrix products, arithmetic and copies ran while one was open for 3% of the time, Pallas kernels for 0%

profile of v3, /device:TPU:1, one launch (start us, length us, event | category | flops | bytes accessed | tf_op | source)
XLA Modules:
  0.0 308.7 jit_solution(12491044865027069944)
XLA Ops:
  0.0 1.8 slice.9
  1.8 1.3 collective-permute-start
  3.2 4.3 %sine_multiply_fusion = (f32[8,128,256]{2,1,0:T(8,128)S(1)}, f32[8,128,256]{2,1,0:T(8,128)S(1)}, f32[8,128,256]{2,1,0:T(8,128)S(1)}) fusion(s32[8,128]{1,0:T(8,128)S(1)} %iota_add_fusion), kind=kLoop, calls=%fused_computation.19 | loop fusion | flops 4456448 | bytes 3149824 | tf_op jit(solution)/shard_map/mul | solution.py:41
  7.4 1.6 fusion.8.bh_ref
  9.0 0.0 copy-start
  9.0 1.7 subtract_convert_fusion.bl_ref
  10.7 0.6 fusion.20
  11.3 7.3 %collective-permute-done = bf16[8,30720]{1,0:T(8,128)(2,1)} collective-permute-done((bf16[8,30720]{1,0:T(8,128)(2,1)}, bf16[8,30720]{1,0:T(8,128)(2,1)}, u32[]{:S(2)}, u32[]{:S(2)}) %collective-permute-start) | collective-permute-done | bytes 491552 | tf_op jit(solution)/shard_map/ppermute | solution.py:22
  18.6 0.0 copy-done
  18.6 1.9 broadcast_select_fusion.xh_ref
  20.5 1.1 broadcast_in_dim.7.wb_ref
  21.5 111.3 %shard_map.28 = bf16[2,8,256,1024]{3,2,1,0:T(8,128)(2,1)} custom-call(bf16[8,524288]{1,0:T(8,128)(2,1)} %xa_ref.1, bf16[8,30720]{1,0:T(8,128)(2,1)} %broadcast_select_fusion.xh_ref, f32[16,8,2048]{2,1,0:T(8,128)} %broadcast_in_dim.7.wb_ref, bf16[8,256,512]{2,1,0:T(8,128)(2,1)} %fusion.8.bh_ref, bf16[8,256,512]{2,1,0:T(8,128)(2,1)} %subtract_convert_fusion.bl_ref), custom_call_target="tpu_custom_call" | custom-call | flops 11408506880 | bytes 25657344 | tf_op jit(solution)/shard_map/pallas_call | solution.py:178
  132.8 8.8 %copy.10 = bf16[512,8,8,128]{3,2,1,0:T(8,128)(2,1)} copy(bf16[512,8,8,128]{3,1,2,0:T(8,128)(2,1)} %bitcast.35) | data formatting | bytes 16777216
  141.6 9.2 %copy.12 = bf16[2,8,2,128,8,128]{5,4,2,1,0,3:T(8,128)(2,1)} copy(bf16[2,8,2,128,8,128]{5,4,3,2,1,0:T(8,128)(2,1)} %bitcast.31) | data formatting | bytes 16777216 | tf_op jit(solution)/shard_map/reshape | solution.py:218
  150.8 106.0 %all_to_all.5 = bf16[128,8,2,2,8,128]{5,4,2,1,3,0:T(8,128)(2,1)} all-to-all(bf16[128,8,2,2,8,128]{5,4,2,1,3,0:T(8,128)(2,1)} %bitcast.32), channel_id=1, replica_groups=mesh['wide'=64,'narrow'=2] {'wide','narrow'}, dimensions={0} | all-to-all | bytes 16777216 | tf_op jit(solution)/shard_map/all_to_all | solution.py:220
  256.8 9.1 %copy.6 = bf16[64,2,8,2,2,8,128]{6,5,4,1,3,0,2:T(8,128)(2,1)} copy(bf16[64,2,8,2,2,8,128]{6,5,3,2,4,1,0:T(8,128)(2,1)} %bitcast.28) | data formatting | bytes 16777216 | tf_op jit(solution)/shard_map/reshape | solution.py:223
  265.9 8.9 %copy.7 = bf16[8,64,8,2,2,2,128]{6,2,5,4,1,0,3:T(8,128)(2,1)} copy(bf16[8,64,8,2,2,2,128]{6,2,3,0,5,4,1:T(8,128)(2,1)} %bitcast.29) | data formatting | bytes 16777216 | tf_op jit(solution)/shard_map/transpose | solution.py:224
  274.8 5.7 %slice_bitcast_fusion = (bf16[8,512,512]{2,1,0:T(8,128)(2,1)}, bf16[8,512,512]{2,1,0:T(8,128)(2,1)}) fusion(bf16[8,512,2,512]{3,1,0,2:T(8,128)(2,1)} %bitcast.30), kind=kLoop, calls=%fused_computation.9 | loop fusion | flops 2097152 | bytes 16777216 | tf_op jit(solution)/shard_map/squeeze | solution.py:229
  280.6 7.8 %maximum_bitcast_fusion = bf16[8,1,512,1024]{3,2,1,0:T(8,128)(2,1)} fusion(bf16[8,512,512]{2,1,0:T(8,128)(2,1)} %get-tuple-element.6, bf16[8,512,512]{2,1,0:T(8,128)(2,1)} %get-tuple-element.5), kind=kLoop, calls=%fused_computation.5 | loop fusion | flops 16777216 | bytes 16777216 | tf_op jit(solution)/shard_map/stack | solution.py:230
  288.3 20.4 %fusion.4 = f32[8,2,512,512]{3,2,1,0:T(8,128)} fusion(bf16[8,512,1024,1]{2,1,3,0:T(8,128)(2,1)} %bitcast.33, bf16[8,1,512,1024]{3,2,1,0:T(8,128)(2,1)} %maximum_bitcast_fusion, bf16[8,1,512,1024]{3,2,1,0:T(8,128)(2,1)} %bitcast.34), kind=kOutput, calls=%fused_computation.4 | convolution fusion | flops 8602517504 | bytes 41943040 | tf_op jit(solution)/shard_map/csik,cjk->csij/dot_general | solution.py:231
  (2 shorter events, 0.0 us)
Async XLA Ops:
  1.8 16.7 %collective-permute-start = (bf16[8,30720]{1,0:T(8,128)(2,1)}, bf16[8,30720]{1,0:T(8,128)(2,1)}, u32[]{:S(2)}, u32[]{:S(2)}) collective-permute-start(bf16[8,30720]{1,0:T(8,128)(2,1)} %slice.9), channel_id=1, source_target_pairs={{1,0},{3,2},{5,4},{7,6},{9,8},{11,10},{13,12},{15,14},{17,16},{19,... | collective-permute-start | bytes 1474568 | tf_op jit(solution)/shard_map/ppermute | solution.py:22
  9.0 9.6 %copy-start = (bf16[8,30720]{1,0:T(8,128)(2,1)S(1)}, bf16[8,30720]{1,0:T(8,128)(2,1)}, u32[]{:S(2)}) copy-start(bf16[8,30720]{1,0:T(8,128)(2,1)} %param.3) | copy-start | bytes 1474564

commit v4 on v3

--- a/solution.py
+++ b/solution.py
@@ -31,31 +31,31 @@
 
 
 def phase_matrices(salt):
-    k1 = jnp.arange(SUB_LEN, dtype=jnp.int32)[None, None, :]
-    c1 = jnp.arange(CHANNELS // PHASES, dtype=jnp.int32)[None, :, None] + salt
+    k1 = jnp.arange(SUB_LEN, dtype=jnp.int32)[None, :, None]
+    c1 = jnp.arange(CHANNELS // PHASES, dtype=jnp.int32)[None, None, :] + salt
     c2 = jnp.arange(PHASES, dtype=jnp.int32)[:, None, None]
     turns = (k1 * (PHASES * c1 + c2)) % FFT_LEN
     angles = (2.0 * jnp.pi / FFT_LEN) * turns.astype(jnp.float32)
     scaling = 1.0 / math.sqrt(FFT_LEN)
     cos_t = jnp.cos(angles) * scaling
     sin_t = jnp.sin(angles) * scaling
-    real_row = jnp.concatenate([cos_t, sin_t], axis=-1)
-    imag_row = jnp.concatenate([-sin_t, cos_t], axis=-1)
-    full = jnp.concatenate([real_row, imag_row], axis=1)
-    high = full.astype(jnp.bfloat16)
-    low = (full - high.astype(jnp.float32)).astype(jnp.bfloat16)
-    return high, low
+    top = jnp.concatenate([cos_t, -sin_t], axis=-1)
+    bottom = jnp.concatenate([sin_t, cos_t], axis=-1)
+    full = jnp.concatenate([top, bottom], axis=1)
+    return split_exact(full)
+
+
+def split_exact(value):
+    scaled = value * 65537.0
+    high = scaled - (scaled - value)
+    low = value - high
+    return high.astype(jnp.bfloat16), low.astype(jnp.bfloat16)
 
 
 def split_parts(value):
     high = value.astype(jnp.bfloat16)
     low = (value - high.astype(jnp.float32)).astype(jnp.bfloat16)
     return high, low
-
-
-def nearest_bf16(value):
-    scaled = value * 65537.0
-    return (scaled - (scaled - value)).astype(jnp.bfloat16)
 
 
 def spectra_kernel(xa_ref, xh_ref, wb_ref, bh_ref, bl_ref, out_ref,
@@ -155,17 +155,16 @@
 
         lax.fori_loop(0, sub_rows // rows_per, butterflies, 0)
 
-        nt = (((1,), (1,)), ((), ()))
         for c2 in range(PHASES):
             depth = SUB_LEN if c2 in (0, PHASES // 2) else 2 * SUB_LEN
             uh = uh_ref[c2, :, 0:depth]
             ul = ul_ref[c2, :, 0:depth]
-            bh = bh_ref[c2, :, 0:depth]
-            bl = bl_ref[c2, :, 0:depth]
-            acc = lax.dot_general(bh, uh, nt, preferred_element_type=jnp.float32)
-            acc = acc + lax.dot_general(bh, ul, nt, preferred_element_type=jnp.float32)
-            acc = acc + lax.dot_general(bl, uh, nt, preferred_element_type=jnp.float32)
-            out_ref[0, c2, :, sub * sub_rows:(sub + 1) * sub_rows] = nearest_bf16(acc)
+            bh = bh_ref[c2, 0:depth, :]
+            bl = bl_ref[c2, 0:depth, :]
+            acc = jnp.dot(uh, bh, preferred_element_type=jnp.float32)
+            acc = acc + jnp.dot(ul, bh, preferred_element_type=jnp.float32)
+            acc = acc + jnp.dot(uh, bl, preferred_element_type=jnp.float32)
+            out_ref[0, c2, :, sub * sub_rows:(sub + 1) * sub_rows] = acc.T.astype(jnp.bfloat16)
 
 
 def pfb_spectra(xa, xh, wb, bh, bl):

time: 310 us -> 310 us (level)
    mul x1 -> x0, other arithmetic: 4.26 us -> none  [phase_matrices(): sin_t = jnp.sin(angles) * scaling]
    neg x0 -> x1, other arithmetic: none -> 4.17 us  [phase_matrices(): top = jnp.concatenate([cos_t, -sin_t], axis=-1)]
    unnamed x3 -> x1, local copies, waits for them, and re-layouts: 8.77 us -> 8.77 us
  transfers between devices with their start and end apart: 1 -> 1, of which waited for: 1 -> 1; matrix products, arithmetic and copies ran while one was open for 3% -> 2% of each run, Pallas kernels for 0% -> 0%
where the time goes in v4:
time: 310 us; the launch traced here: 309 us
  Pallas kernels  112 us (36%)
  blocking collectives  106 us (34%)
  local copies, waits for them, and re-layouts  38.9 us (13%)
  other arithmetic  22.7 us (7%)
  matrix products  20.4 us (7%)
  waiting for transfers between devices  8.08 us (3%)
    pallas_call x1, Pallas kernels, pfb_spectra(): pl.pallas_call(spectra_kernel, out_shape=jax.ShapeDtypeStruct((steps, PHA...  112 us
    all_to_all x1, blocking collectives, shards(): got = lax.all_to_all(spec, ('wide', 'narrow'), 0, 0, tiled=True)  106 us
    dot_general x1, matrix products, shards(): jnp.einsum('csik,cjk->csij', lhs, both, preferred_element_type=jnp.float32)  20.4 us
    reshape x1, local copies, waits for them, and re-layouts, shards(): out = out.reshape(steps, PHASES, 2, c1_len, local_inputs, CHUNK)  9.19 us
    reshape x1, local copies, waits for them, and re-layouts, shards(): got = got.reshape(n_wide, n_narrow, PHASES, 2, steps, local_inputs, CHUNK)  9.07 us
    transpose x1, local copies, waits for them, and re-layouts, shards(): got = jnp.transpose(got, (2, 0, 5, 3, 1, 4, 6))  8.95 us
    unnamed x1, local copies, waits for them, and re-layouts  8.77 us
    ppermute x1, waiting for transfers between devices, from_behind(): return lax.ppermute(x, axis, pairs)  8.08 us
  transfers between devices with their start and end apart: 1, of which 1 were waited for; matrix products, arithmetic and copies ran while one was open for 2% of the time, Pallas kernels for 0%

profile of v4, /device:TPU:1, one launch (start us, length us, event | category | flops | bytes accessed | tf_op | source)
XLA Modules:
  0.0 309.2 jit_solution(8853453021624895468)
XLA Ops:
  0.0 1.8 slice.9
  1.8 1.3 collective-permute-start
  3.2 4.2 %fusion.17 = (f32[8,256,128]{2,1,0:T(8,128)S(1)}, f32[8,256,128]{2,1,0:T(8,128)S(1)}, f32[8,256,128]{2,1,0:T(8,128)S(1)}) fusion(s32[8,128]{1,0:T(8,128)S(1)} %iota_add_fusion), kind=kLoop, calls=%fused_computation.27 | loop fusion | flops 4456448 | bytes 3149824 | tf_op jit(solution)/shard_map/neg | solution.py:42
  7.3 0.6 fusion.22
  8.0 2.5 fusion.9
  10.5 8.1 %collective-permute-done = bf16[8,30720]{1,0:T(8,128)(2,1)} collective-permute-done((bf16[8,30720]{1,0:T(8,128)(2,1)}, bf16[8,30720]{1,0:T(8,128)(2,1)}, u32[]{:S(2)}, u32[]{:S(2)}) %collective-permute-start) | collective-permute-done | bytes 491552 | tf_op jit(solution)/shard_map/ppermute | solution.py:22
  18.6 1.9 broadcast_select_fusion.xh_ref
  20.5 1.1 broadcast_in_dim.7.wb_ref
  21.5 111.8 %shard_map.28 = bf16[2,8,256,1024]{3,2,1,0:T(8,128)(2,1)} custom-call(bf16[8,524288]{1,0:T(8,128)(2,1)} %xa_ref.1, bf16[8,30720]{1,0:T(8,128)(2,1)} %broadcast_select_fusion.xh_ref, f32[16,8,2048]{2,1,0:T(8,128)} %broadcast_in_dim.7.wb_ref, bf16[8,512,256]{2,1,0:T(8,128)(2,1)} %get-tuple-element.8.bh_ref, bf16[8,512,256]{2,1,0:T(8,128)(2,1)} %get-tuple-element.7.bl_ref), custom_call_target="tpu_custom_call" | custom-call | flops 11408506880 | bytes 25657344 | tf_op jit(solution)/shard_map/pallas_call | solution.py:177
  133.3 8.8 %copy.10 = bf16[512,8,8,128]{3,2,1,0:T(8,128)(2,1)} copy(bf16[512,8,8,128]{3,1,2,0:T(8,128)(2,1)} %bitcast.35) | data formatting | bytes 16777216
  142.1 9.2 %copy.12 = bf16[2,8,2,128,8,128]{5,4,2,1,0,3:T(8,128)(2,1)} copy(bf16[2,8,2,128,8,128]{5,4,3,2,1,0:T(8,128)(2,1)} %bitcast.31) | data formatting | bytes 16777216 | tf_op jit(solution)/shard_map/reshape | solution.py:217
  151.3 106.1 %all_to_all.5 = bf16[128,8,2,2,8,128]{5,4,2,1,3,0:T(8,128)(2,1)} all-to-all(bf16[128,8,2,2,8,128]{5,4,2,1,3,0:T(8,128)(2,1)} %bitcast.32), channel_id=1, replica_groups=mesh['wide'=64,'narrow'=2] {'wide','narrow'}, dimensions={0} | all-to-all | bytes 16777216 | tf_op jit(solution)/shard_map/all_to_all | solution.py:219
  257.3 9.1 %copy.6 = bf16[64,2,8,2,2,8,128]{6,5,4,1,3,0,2:T(8,128)(2,1)} copy(bf16[64,2,8,2,2,8,128]{6,5,3,2,4,1,0:T(8,128)(2,1)} %bitcast.28) | data formatting | bytes 16777216 | tf_op jit(solution)/shard_map/reshape | solution.py:222
  266.4 8.9 %copy.7 = bf16[8,64,8,2,2,2,128]{6,2,5,4,1,0,3:T(8,128)(2,1)} copy(bf16[8,64,8,2,2,2,128]{6,2,3,0,5,4,1:T(8,128)(2,1)} %bitcast.29) | data formatting | bytes 16777216 | tf_op jit(solution)/shard_map/transpose | solution.py:223
  275.4 5.7 %slice_bitcast_fusion = (bf16[8,512,512]{2,1,0:T(8,128)(2,1)}, bf16[8,512,512]{2,1,0:T(8,128)(2,1)}) fusion(bf16[8,512,2,512]{3,1,0,2:T(8,128)(2,1)} %bitcast.30), kind=kLoop, calls=%fused_computation.13 | loop fusion | flops 2097152 | bytes 16777216 | tf_op jit(solution)/shard_map/squeeze | solution.py:228
  281.1 7.8 %maximum_bitcast_fusion = bf16[8,1,512,1024]{3,2,1,0:T(8,128)(2,1)} fusion(bf16[8,512,512]{2,1,0:T(8,128)(2,1)} %get-tuple-element.6, bf16[8,512,512]{2,1,0:T(8,128)(2,1)} %get-tuple-element.5), kind=kLoop, calls=%fused_computation.5 | loop fusion | flops 16777216 | bytes 16777216 | tf_op jit(solution)/shard_map/stack | solution.py:229
  288.8 20.4 %fusion.4 = f32[8,2,512,512]{3,2,1,0:T(8,128)} fusion(bf16[8,512,1024,1]{2,1,3,0:T(8,128)(2,1)} %bitcast.33, bf16[8,1,512,1024]{3,2,1,0:T(8,128)(2,1)} %maximum_bitcast_fusion, bf16[8,1,512,1024]{3,2,1,0:T(8,128)(2,1)} %bitcast.34), kind=kOutput, calls=%fused_computation.4 | convolution fusion | flops 8602517504 | bytes 41943040 | tf_op jit(solution)/shard_map/csik,cjk->csij/dot_general | solution.py:230
  (2 shorter events, 0.0 us)
Async XLA Ops:
  1.8 16.7 %collective-permute-start = (bf16[8,30720]{1,0:T(8,128)(2,1)}, bf16[8,30720]{1,0:T(8,128)(2,1)}, u32[]{:S(2)}, u32[]{:S(2)}) collective-permute-start(bf16[8,30720]{1,0:T(8,128)(2,1)} %slice.9), channel_id=1, source_target_pairs={{1,0},{3,2},{5,4},{7,6},{9,8},{11,10},{13,12},{15,14},{17,16},{19,... | collective-permute-start | bytes 1474568 | tf_op jit(solution)/shard_map/ppermute | solution.py:22

commit v5 on v4

--- a/solution.py
+++ b/solution.py
@@ -96,13 +96,13 @@
         taps = [wb_ref[p, :, lanes] for p in range(TAPS)]
 
         def filt(ml, _):
-            acc = taps[0] * xf_ref[ml, :, lanes]
-            for p in range(1, TAPS):
-                acc = acc + taps[p] * xf_ref[ml + p, :, lanes]
-            f_ref[lane_at, pl.ds(ml, n_in, stride=CHUNK), :] = acc
-            return 0
-
-        lax.fori_loop(0, CHUNK, filt, 0)
+            terms = [taps[p] * xf_ref[ml + p, :, lanes] for p in range(TAPS)]
+            while len(terms) > 1:
+                terms = [terms[j] + terms[j + 1] for j in range(0, len(terms), 2)]
+            f_ref[lane_at, pl.ds(ml, n_in, stride=CHUNK), :] = terms[0]
+            return 0
+
+        lax.fori_loop(0, CHUNK, filt, 0, unroll=4)
 
     half = 1.0 / math.sqrt(2.0)
     rows_per = 16

time: 310 us -> 256 us (0.83)
  Pallas kernels: 112 us -> 57.2 us
    pallas_call x1, Pallas kernels: 112 us -> 57.2 us  [pfb_spectra(): pl.pallas_call(spectra_kernel, out_shape=jax.ShapeDtypeStruct((steps, PHA...]
  transfers between devices with their start and end apart: 1 -> 1, of which waited for: 1 -> 1; matrix products, arithmetic and copies ran while one was open for 2% -> 3% of each run, Pallas kernels for 0% -> 0%
where the time goes in v5:
time: 256 us; the launch traced here: 255 us
  blocking collectives  106 us (41%)
  Pallas kernels  57.2 us (22%)
  local copies, waits for them, and re-layouts  38.9 us (15%)
  other arithmetic  22.7 us (9%)
  matrix products  20.4 us (8%)
  waiting for transfers between devices  8.08 us (3%)
    all_to_all x1, blocking collectives, shards(): got = lax.all_to_all(spec, ('wide', 'narrow'), 0, 0, tiled=True)  106 us
    pallas_call x1, Pallas kernels, pfb_spectra(): pl.pallas_call(spectra_kernel, out_shape=jax.ShapeDtypeStruct((steps, PHA...  57.2 us
    dot_general x1, matrix products, shards(): jnp.einsum('csik,cjk->csij', lhs, both, preferred_element_type=jnp.float32)  20.4 us
    reshape x1, local copies, waits for them, and re-layouts, shards(): out = out.reshape(steps, PHASES, 2, c1_len, local_inputs, CHUNK)  9.19 us
    reshape x1, local copies, waits for them, and re-layouts, shards(): got = got.reshape(n_wide, n_narrow, PHASES, 2, steps, local_inputs, CHUNK)  9.07 us
    transpose x1, local copies, waits for them, and re-layouts, shards(): got = jnp.transpose(got, (2, 0, 5, 3, 1, 4, 6))  8.95 us
    unnamed x1, local copies, waits for them, and re-layouts  8.77 us
    ppermute x1, waiting for transfers between devices, from_behind(): return lax.ppermute(x, axis, pairs)  8.08 us
  transfers between devices with their start and end apart: 1, of which 1 were waited for; matrix products, arithmetic and copies ran while one was open for 3% of the time, Pallas kernels for 0%

profile of v5, /device:TPU:1, one launch (start us, length us, event | category | flops | bytes accessed | tf_op | source)
XLA Modules:
  0.0 254.7 jit_solution(17487242087554671216)
XLA Ops:
  0.0 1.8 slice.9
  1.8 1.3 collective-permute-start
  3.2 4.2 %fusion.17 = (f32[8,256,128]{2,1,0:T(8,128)S(1)}, f32[8,256,128]{2,1,0:T(8,128)S(1)}, f32[8,256,128]{2,1,0:T(8,128)S(1)}) fusion(s32[8,128]{1,0:T(8,128)S(1)} %iota_add_fusion), kind=kLoop, calls=%fused_computation.27 | loop fusion | flops 4456448 | bytes 3149824 | tf_op jit(solution)/shard_map/neg | solution.py:42
  7.3 0.6 fusion.22
  8.0 2.5 fusion.9
  10.5 8.1 %collective-permute-done = bf16[8,30720]{1,0:T(8,128)(2,1)} collective-permute-done((bf16[8,30720]{1,0:T(8,128)(2,1)}, bf16[8,30720]{1,0:T(8,128)(2,1)}, u32[]{:S(2)}, u32[]{:S(2)}) %collective-permute-start) | collective-permute-done | bytes 491552 | tf_op jit(solution)/shard_map/ppermute | solution.py:22
  18.6 1.9 broadcast_select_fusion.xh_ref
  20.5 1.1 broadcast_in_dim.7.wb_ref
  21.5 57.2 %shard_map.28 = bf16[2,8,256,1024]{3,2,1,0:T(8,128)(2,1)} custom-call(bf16[8,524288]{1,0:T(8,128)(2,1)} %xa_ref.1, bf16[8,30720]{1,0:T(8,128)(2,1)} %broadcast_select_fusion.xh_ref, f32[16,8,2048]{2,1,0:T(8,128)} %broadcast_in_dim.7.wb_ref, bf16[8,512,256]{2,1,0:T(8,128)(2,1)} %get-tuple-element.8.bh_ref, bf16[8,512,256]{2,1,0:T(8,128)(2,1)} %get-tuple-element.7.bl_ref), custom_call_target="tpu_custom_call" | custom-call | flops 11408506880 | bytes 25657344 | tf_op jit(solution)/shard_map/pallas_call | solution.py:177
  78.8 8.8 %copy.10 = bf16[512,8,8,128]{3,2,1,0:T(8,128)(2,1)} copy(bf16[512,8,8,128]{3,1,2,0:T(8,128)(2,1)} %bitcast.35) | data formatting | bytes 16777216
  87.5 9.2 %copy.12 = bf16[2,8,2,128,8,128]{5,4,2,1,0,3:T(8,128)(2,1)} copy(bf16[2,8,2,128,8,128]{5,4,3,2,1,0:T(8,128)(2,1)} %bitcast.31) | data formatting | bytes 16777216 | tf_op jit(solution)/shard_map/reshape | solution.py:217
  96.7 106.1 %all_to_all.5 = bf16[128,8,2,2,8,128]{5,4,2,1,3,0:T(8,128)(2,1)} all-to-all(bf16[128,8,2,2,8,128]{5,4,2,1,3,0:T(8,128)(2,1)} %bitcast.32), channel_id=1, replica_groups=mesh['wide'=64,'narrow'=2] {'wide','narrow'}, dimensions={0} | all-to-all | bytes 16777216 | tf_op jit(solution)/shard_map/all_to_all | solution.py:219
  202.8 9.1 %copy.6 = bf16[64,2,8,2,2,8,128]{6,5,4,1,3,0,2:T(8,128)(2,1)} copy(bf16[64,2,8,2,2,8,128]{6,5,3,2,4,1,0:T(8,128)(2,1)} %bitcast.28) | data formatting | bytes 16777216 | tf_op jit(solution)/shard_map/reshape | solution.py:222
  211.9 8.9 %copy.7 = bf16[8,64,8,2,2,2,128]{6,2,5,4,1,0,3:T(8,128)(2,1)} copy(bf16[8,64,8,2,2,2,128]{6,2,3,0,5,4,1:T(8,128)(2,1)} %bitcast.29) | data formatting | bytes 16777216 | tf_op jit(solution)/shard_map/transpose | solution.py:223
  220.8 5.7 %slice_bitcast_fusion = (bf16[8,512,512]{2,1,0:T(8,128)(2,1)}, bf16[8,512,512]{2,1,0:T(8,128)(2,1)}) fusion(bf16[8,512,2,512]{3,1,0,2:T(8,128)(2,1)} %bitcast.30), kind=kLoop, calls=%fused_computation.13 | loop fusion | flops 2097152 | bytes 16777216 | tf_op jit(solution)/shard_map/squeeze | solution.py:228
  226.5 7.8 %maximum_bitcast_fusion = bf16[8,1,512,1024]{3,2,1,0:T(8,128)(2,1)} fusion(bf16[8,512,512]{2,1,0:T(8,128)(2,1)} %get-tuple-element.6, bf16[8,512,512]{2,1,0:T(8,128)(2,1)} %get-tuple-element.5), kind=kLoop, calls=%fused_computation.5 | loop fusion | flops 16777216 | bytes 16777216 | tf_op jit(solution)/shard_map/stack | solution.py:229
  234.3 20.4 %fusion.4 = f32[8,2,512,512]{3,2,1,0:T(8,128)} fusion(bf16[8,512,1024,1]{2,1,3,0:T(8,128)(2,1)} %bitcast.33, bf16[8,1,512,1024]{3,2,1,0:T(8,128)(2,1)} %maximum_bitcast_fusion, bf16[8,1,512,1024]{3,2,1,0:T(8,128)(2,1)} %bitcast.34), kind=kOutput, calls=%fused_computation.4 | convolution fusion | flops 8602517504 | bytes 41943040 | tf_op jit(solution)/shard_map/csik,cjk->csij/dot_general | solution.py:230
  (2 shorter events, 0.0 us)
Async XLA Ops:
  1.8 16.7 %collective-permute-start = (bf16[8,30720]{1,0:T(8,128)(2,1)}, bf16[8,30720]{1,0:T(8,128)(2,1)}, u32[]{:S(2)}, u32[]{:S(2)}) collective-permute-start(bf16[8,30720]{1,0:T(8,128)(2,1)} %slice.9), channel_id=1, source_target_pairs={{1,0},{3,2},{5,4},{7,6},{9,8},{11,10},{13,12},{15,14},{17,16},{19,... | collective-permute-start | bytes 1474568 | tf_op jit(solution)/shard_map/ppermute | solution.py:22

commit v6 on v5

--- a/solution.py
+++ b/solution.py
@@ -199,6 +199,53 @@
     )(xa, xh, wb, bh, bl)
 
 
+def gram_kernel(n_narrow, g_ref, out_ref, l_ref):
+    n_src = g_ref.shape[0]
+    steps = g_ref.shape[3]
+    seg = g_ref.shape[5]
+    n_in = g_ref.shape[4]
+
+    def gather(w, _):
+        row = pl.multiple_of(w * n_in, n_in)
+        for n in range(n_narrow):
+            for ri in range(2):
+                for s in range(steps):
+                    col = ((ri * n_narrow + n) * steps + s) * seg
+                    l_ref[pl.ds(row, n_in), col:col + seg] = g_ref[w * n_narrow + n, 0, ri, s].astype(jnp.float32)
+        return 0
+
+    lax.fori_loop(0, n_src // n_narrow, gather, 0)
+    both = l_ref[...].astype(jnp.bfloat16)
+    half = both.shape[1] // 2
+    turned = jnp.concatenate([both[:, half:], -both[:, :half]], axis=1)
+    nt = (((1,), (1,)), ((), ()))
+    scale = 1.0 / half
+    out_ref[0, 0] = lax.dot_general(both, both, nt, preferred_element_type=jnp.float32) * scale
+    out_ref[0, 1] = lax.dot_general(turned, both, nt, preferred_element_type=jnp.float32) * scale
+
+
+def visibilities(got, n_narrow):
+    n_src, phases, parts, steps, n_in, seg = got.shape
+    all_inputs = n_src // n_narrow * n_in
+    depth = parts * n_narrow * steps * seg
+    return pl.pallas_call(
+        functools.partial(gram_kernel, n_narrow),
+        out_shape=jax.ShapeDtypeStruct((phases, 2, all_inputs, all_inputs), jnp.float32),
+        grid=(phases,),
+        in_specs=[pl.BlockSpec((n_src, 1, parts, steps, n_in, seg), lambda c: (0, c, 0, 0, 0, 0))],
+        out_specs=pl.BlockSpec((1, 2, all_inputs, all_inputs), lambda c: (c, 0, 0, 0)),
+        scratch_shapes=[pltpu.VMEM((all_inputs, depth), jnp.float32)],
+        compiler_params=pltpu.CompilerParams(
+            dimension_semantics=("arbitrary",), vmem_limit_bytes=48 * 1024 * 1024
+        ),
+        cost_estimate=pl.CostEstimate(
+            flops=phases * 4 * all_inputs * all_inputs * depth,
+            transcendentals=0,
+            bytes_accessed=got.size * 2 + phases * 2 * all_inputs * all_inputs * 4,
+        ),
+    )(got)
+
+
 def shards(voltages, following):
     local_inputs, local_span = voltages.shape
     local_spec = local_span // FFT_LEN
@@ -217,18 +264,7 @@
     out = out.reshape(steps, PHASES, 2, c1_len, local_inputs, CHUNK)
     spec = jnp.transpose(out, (3, 1, 2, 0, 4, 5))
     got = lax.all_to_all(spec, ("wide", "narrow"), 0, 0, tiled=True)
-    n_wide = lax.axis_size("wide")
-    n_narrow = lax.axis_size("narrow")
-    got = got.reshape(n_wide, n_narrow, PHASES, 2, steps, local_inputs, CHUNK)
-    got = jnp.transpose(got, (2, 0, 5, 3, 1, 4, 6))
-    all_inputs = n_wide * local_inputs
-    time_len = n_narrow * local_spec
-    got = got.reshape(PHASES, all_inputs, 2, time_len)
-    both = got.reshape(PHASES, all_inputs, 2 * time_len)
-    turned = jnp.concatenate([got[:, :, 1], -got[:, :, 0]], axis=-1)
-    lhs = jnp.stack([both, turned], axis=1)
-    vis = jnp.einsum("csik,cjk->csij", lhs, both, preferred_element_type=jnp.float32)
-    return vis * (1.0 / time_len)
+    return visibilities(got, lax.axis_size("narrow"))
 
 
 def solution(mesh):

time: 256 us -> 222 us (0.87)
  matrix products: 20.4 us -> 0 us
  local copies, waits for them, and re-layouts: 38.9 us -> 20.9 us
  Pallas kernels: 57.2 us -> 74.6 us
  other arithmetic: 22.7 us -> 9.25 us
    dot_general x1 -> x0, matrix products: 20.4 us -> none  [shards(): jnp.einsum('csik,cjk->csij', lhs, both, preferred_element_type=jnp.float32)]
    pallas_call x0 -> x1, Pallas kernels: none -> 17.4 us  [visibilities(): pl.pallas_call(functools.partial(gram_kernel, n_narrow), out_shape=jax.Sh...]
    reshape x1 -> x0, local copies, waits for them, and re-layouts: 9.07 us -> none  [shards(): got = got.reshape(n_wide, n_narrow, PHASES, 2, steps, local_inputs, CHUNK)]
    transpose x1 -> x0, local copies, waits for them, and re-layouts: 8.95 us -> none  [shards(): got = jnp.transpose(got, (2, 0, 5, 3, 1, 4, 6))]
    another operation x1 -> x0, other arithmetic: 7.78 us -> none  [shards(): lhs = jnp.stack([both, turned], axis=1)]
    squeeze x1 -> x0, other arithmetic: 5.72 us -> none  [shards(): turned = jnp.concatenate([got[:, :, 1], -got[:, :, 0]], axis=-1)]
    unnamed x1 -> x3, local copies, waits for them, and re-layouts: 8.77 us -> 8.77 us
where the time goes in v6:
time: 222 us; the launch traced here: 220 us
  blocking collectives  106 us (48%)
  Pallas kernels  74.6 us (34%)
  local copies, waits for them, and re-layouts  20.9 us (9%)
  other arithmetic  9.25 us (4%)
  waiting for transfers between devices  8.07 us (4%)
    all_to_all x1, blocking collectives, shards(): got = lax.all_to_all(spec, ('wide', 'narrow'), 0, 0, tiled=True)  106 us
    pallas_call x1, Pallas kernels, pfb_spectra(): pl.pallas_call(spectra_kernel, out_shape=jax.ShapeDtypeStruct((steps, PHA...  57.2 us
    pallas_call x1, Pallas kernels, visibilities(): pl.pallas_call(functools.partial(gram_kernel, n_narrow), out_shape=jax.Sh...  17.4 us
    reshape x1, local copies, waits for them, and re-layouts, shards(): out = out.reshape(steps, PHASES, 2, c1_len, local_inputs, CHUNK)  9.18 us
    unnamed x3, local copies, waits for them, and re-layouts  8.77 us
    ppermute x1, waiting for transfers between devices, from_behind(): return lax.ppermute(x, axis, pairs)  8.07 us
  transfers between devices with their start and end apart: 1, of which 1 were waited for; matrix products, arithmetic and copies ran while one was open for 3% of the time, Pallas kernels for 0%

profile of v6, /device:TPU:1, one launch (start us, length us, event | category | flops | bytes accessed | tf_op | source)
XLA Modules:
  0.0 220.1 jit_solution(7090629960268785655)
XLA Ops:
  0.0 1.8 slice.3
  1.8 1.3 collective-permute-start
  3.2 4.2 %fusion.9 = (f32[8,256,128]{2,1,0:T(8,128)S(1)}, f32[8,256,128]{2,1,0:T(8,128)S(1)}, f32[8,256,128]{2,1,0:T(8,128)S(1)}) fusion(s32[8,128]{1,0:T(8,128)S(1)} %iota_add_fusion), kind=kLoop, calls=%fused_computation.18 | loop fusion | flops 4456448 | bytes 3149824 | tf_op jit(solution)/shard_map/neg | solution.py:42
  7.3 0.0 copy-start
  7.3 0.6 fusion.14
  8.0 2.5 %fusion.2 = (bf16[8,512,256]{2,1,0:T(8,128)(2,1)}, bf16[8,512,256]{2,1,0:T(8,128)(2,1)}) fusion(f32[8,256,128]{2,1,0:T(8,128)S(1)} %get-tuple-element.9, f32[8,256,128]{2,1,0:T(8,128)S(1)} %get-tuple-element.8, f32[8,256,128]{2,1,0:T(8,128)S(1)} %get-tuple-element.7), kind=kLoop, calls=%fused_computation.4 | loop fusion | flops 9437184 | bytes 7340032 | tf_op jit(solution)/shard_map/convert_element_type | solution.py:52
  10.5 8.1 %collective-permute-done = bf16[8,30720]{1,0:T(8,128)(2,1)} collective-permute-done((bf16[8,30720]{1,0:T(8,128)(2,1)}, bf16[8,30720]{1,0:T(8,128)(2,1)}, u32[]{:S(2)}, u32[]{:S(2)}) %collective-permute-start) | collective-permute-done | bytes 491552 | tf_op jit(solution)/shard_map/ppermute | solution.py:22
  18.6 0.0 copy-done
  18.6 1.9 broadcast_select_fusion.xh_ref
  20.5 1.1 broadcast_in_dim.7.wb_ref
  21.6 57.2 %shard_map.28 = bf16[2,8,256,1024]{3,2,1,0:T(8,128)(2,1)} custom-call(bf16[8,524288]{1,0:T(8,128)(2,1)} %xa_ref.1, bf16[8,30720]{1,0:T(8,128)(2,1)} %broadcast_select_fusion.xh_ref, f32[16,8,2048]{2,1,0:T(8,128)} %broadcast_in_dim.7.wb_ref, bf16[8,512,256]{2,1,0:T(8,128)(2,1)} %get-tuple-element.6.bh_ref, bf16[8,512,256]{2,1,0:T(8,128)(2,1)} %get-tuple-element.5.bl_ref), custom_call_target="tpu_custom_call" | custom-call | flops 11408506880 | bytes 25657344 | tf_op jit(solution)/shard_map/pallas_call | solution.py:177
  78.8 8.8 %copy.4 = bf16[512,8,8,128]{3,2,1,0:T(8,128)(2,1)} copy(bf16[512,8,8,128]{3,1,2,0:T(8,128)(2,1)} %bitcast.10) | data formatting | bytes 16777216
  87.6 9.2 %copy.6 = bf16[2,8,2,128,8,128]{5,4,0,2,1,3:T(8,128)(2,1)} copy(bf16[2,8,2,128,8,128]{5,4,3,2,1,0:T(8,128)(2,1)} %bitcast.8) | data formatting | bytes 16777216 | tf_op jit(solution)/shard_map/reshape | solution.py:264
  96.7 106.0 %all_to_all.5.g_ref = bf16[128,8,2,2,8,128]{5,4,3,2,1,0:T(8,128)(2,1)} all-to-all(bf16[128,8,2,2,8,128]{5,4,3,2,1,0:T(8,128)(2,1)} %bitcast.9), channel_id=1, replica_groups=mesh['wide'=64,'narrow'=2] {'wide','narrow'}, dimensions={0} | all-to-all | bytes 16777216 | tf_op jit(solution)/shard_map/all_to_all | solution.py:266
  202.8 17.4 %shard_map.29 = f32[8,2,512,512]{3,2,1,0:T(8,128)} custom-call(bf16[128,8,2,2,8,128]{5,4,3,2,1,0:T(8,128)(2,1)} %all_to_all.5.g_ref), custom_call_target="tpu_custom_call" | custom-call | flops 8589934592 | bytes 25165824 | tf_op jit(solution)/shard_map/pallas_call | solution.py:231
  (2 shorter events, 0.0 us)
Async XLA Ops:
  1.8 16.7 %collective-permute-start = (bf16[8,30720]{1,0:T(8,128)(2,1)}, bf16[8,30720]{1,0:T(8,128)(2,1)}, u32[]{:S(2)}, u32[]{:S(2)}) collective-permute-start(bf16[8,30720]{1,0:T(8,128)(2,1)} %slice.3), channel_id=1, source_target_pairs={{1,0},{3,2},{5,4},{7,6},{9,8},{11,10},{13,12},{15,14},{17,16},{19,... | collective-permute-start | bytes 1474568 | tf_op jit(solution)/shard_map/ppermute | solution.py:22
  7.3 11.3 %copy-start = (bf16[8,30720]{1,0:T(8,128)(2,1)S(1)}, bf16[8,30720]{1,0:T(8,128)(2,1)}, u32[]{:S(2)}) copy-start(bf16[8,30720]{1,0:T(8,128)(2,1)} %param.3) | copy-start | bytes 1474564

commit v7 on v6

--- a/solution.py
+++ b/solution.py
@@ -58,37 +58,28 @@
     return high, low
 
 
-def spectra_kernel(xa_ref, xh_ref, wb_ref, bh_ref, bl_ref, out_ref,
-                   xf_ref, f_ref, uh_ref, ul_ref):
-    step = pl.program_id(0)
-    last = pl.num_programs(0) - 1
-    halo = TAPS - 1
+def spectra_kernel(with_halo, *refs):
+    if with_halo:
+        xa_ref, xh_ref, wb_ref, bh_ref, bl_ref, _, out_ref, xf_ref, f_ref, uh_ref, ul_ref = refs
+    else:
+        xa_ref, wb_ref, bh_ref, bl_ref, out_ref, xf_ref, f_ref, uh_ref, ul_ref = refs
+        xh_ref = xa_ref
     n_in = xa_ref.shape[0]
+    own = CHUNK if with_halo else CHUNK + TAPS - 1
 
     def load_block(q_local, _):
-        q = step * CHUNK + q_local
-        start = pl.multiple_of(q * FFT_LEN, FFT_LEN)
+        start = pl.multiple_of(q_local * FFT_LEN, FFT_LEN)
         xf_ref[q_local] = xa_ref[:, pl.ds(start, FFT_LEN)].astype(jnp.float32)
         return 0
 
-    lax.fori_loop(0, CHUNK, load_block, 0)
-
-    @pl.when(step < last)
-    def _():
-        def body(j, _):
-            q = (step + 1) * CHUNK + j
-            start = pl.multiple_of(q * FFT_LEN, FFT_LEN)
-            xf_ref[CHUNK + j] = xa_ref[:, pl.ds(start, FFT_LEN)].astype(jnp.float32)
-            return 0
-        lax.fori_loop(0, halo, body, 0)
-
-    @pl.when(step == last)
-    def _():
+    lax.fori_loop(0, own, load_block, 0)
+
+    if with_halo:
         def body(j, _):
             start = pl.multiple_of(j * FFT_LEN, FFT_LEN)
             xf_ref[CHUNK + j] = xh_ref[:, pl.ds(start, FFT_LEN)].astype(jnp.float32)
             return 0
-        lax.fori_loop(0, halo, body, 0)
+        lax.fori_loop(0, TAPS - 1, body, 0)
 
     lane_w = 128
     for lane_at in range(FFT_LEN // lane_w):
@@ -167,25 +158,36 @@
             out_ref[0, c2, :, sub * sub_rows:(sub + 1) * sub_rows] = acc.T.astype(jnp.bfloat16)
 
 
-def pfb_spectra(xa, xh, wb, bh, bl):
+def pfb_chunk(xa, xh, wb, bh, bl, chunk_at, prev):
     n_in, span = xa.shape
-    n_spec = span // FFT_LEN
-    steps = n_spec // CHUNK
     rows = CHUNK * n_in
-    flops = 2 * steps * rows * 3 * SUB_LEN * 2 * SUB_LEN * 7 + 2 * n_in * n_spec * FFT_LEN * TAPS
-    bytes_accessed = xa.size * 2 + xh.size * 2 + steps * PHASES * rows * 2 * SUB_LEN * 2
+    with_halo = xh is not None
+    lanes = CHUNK * FFT_LEN if with_halo else (CHUNK + TAPS - 1) * FFT_LEN
+    flops = 2 * rows * 3 * SUB_LEN * 2 * SUB_LEN * 7 + 2 * n_in * CHUNK * FFT_LEN * TAPS
+    bytes_accessed = n_in * lanes * 2 + PHASES * rows * 2 * SUB_LEN * 2
+    xa_spec = pl.BlockSpec((n_in, lanes), lambda s: (0, chunk_at))
+    const3 = lambda s: (0, 0, 0)
+    in_specs = [pl.BlockSpec(xa_spec.block_shape, xa_spec.index_map, pipeline_mode=pl.Buffered(1))]
+    operands = [xa]
+    if with_halo:
+        in_specs.append(pl.BlockSpec(xh.shape, lambda s: (0, 0), pipeline_mode=pl.Buffered(1)))
+        operands.append(xh)
+    for arr in (wb, bh, bl):
+        in_specs.append(pl.BlockSpec(arr.shape, const3, pipeline_mode=pl.Buffered(1)))
+        operands.append(arr)
+    aliases = {}
+    if with_halo:
+        in_specs.append(pl.BlockSpec(memory_space=pl.ANY))
+        operands.append(prev)
+        aliases = {len(operands) - 1: 0}
+    steps = span // FFT_LEN // CHUNK
     return pl.pallas_call(
-        spectra_kernel,
+        functools.partial(spectra_kernel, with_halo),
         out_shape=jax.ShapeDtypeStruct((steps, PHASES, 2 * CHANNELS // PHASES, rows), jnp.bfloat16),
-        grid=(steps,),
-        in_specs=[
-            pl.BlockSpec((n_in, span), lambda s: (0, 0), pipeline_mode=pl.Buffered(1)),
-            pl.BlockSpec(xh.shape, lambda s: (0, 0), pipeline_mode=pl.Buffered(1)),
-            pl.BlockSpec(wb.shape, lambda s: (0, 0, 0), pipeline_mode=pl.Buffered(1)),
-            pl.BlockSpec(bh.shape, lambda s: (0, 0, 0), pipeline_mode=pl.Buffered(1)),
-            pl.BlockSpec(bl.shape, lambda s: (0, 0, 0), pipeline_mode=pl.Buffered(1)),
-        ],
-        out_specs=pl.BlockSpec((1, PHASES, 2 * CHANNELS // PHASES, rows), lambda s: (s, 0, 0, 0)),
+        grid=(1,),
+        in_specs=in_specs,
+        out_specs=pl.BlockSpec((1, PHASES, 2 * CHANNELS // PHASES, rows), lambda s: (chunk_at, 0, 0, 0)),
+        input_output_aliases=aliases,
         scratch_shapes=[
             pltpu.VMEM((CHUNK + TAPS - 1, n_in, FFT_LEN), jnp.float32),
             pltpu.VMEM((FFT_LEN // 128, rows, 128), jnp.float32),
@@ -196,7 +198,14 @@
             dimension_semantics=("arbitrary",), vmem_limit_bytes=62 * 1024 * 1024
         ),
         cost_estimate=pl.CostEstimate(flops=flops, transcendentals=0, bytes_accessed=bytes_accessed),
-    )(xa, xh, wb, bh, bl)
+    )(*operands)
+
+
+def pfb_spectra(xa, xh, wb, bh, bl):
+    n_spec = xa.shape[1] // FFT_LEN
+    steps = n_spec // CHUNK
+    first = pfb_chunk(xa, None, wb, bh, bl, 0, None)
+    return pfb_chunk(xa, xh, wb, bh, bl, steps - 1, first)
 
 
 def gram_kernel(n_narrow, g_ref, out_ref, l_ref):

time: 222 us -> 222 us (level)
  waiting for transfers between devices: 8.07 us -> 0.01 us
  Pallas kernels: 74.6 us -> 79.3 us
  blocking collectives: 106 us -> 109 us
    ppermute x1, waiting for transfers between devices: 8.07 us -> 0.01 us  [from_behind(): return lax.ppermute(x, axis, pairs)]
    pallas_call x1 -> x2, Pallas kernels: 57.2 us -> 61.9 us  [pfb_chunk(): pl.pallas_call(functools.partial(spectra_kernel, with_halo), out_shape=ja...]
    all_to_all x1, blocking collectives: 106 us -> 109 us  [shards(): got = lax.all_to_all(spec, ('wide', 'narrow'), 0, 0, tiled=True)]
  transfers between devices with their start and end apart: 1 -> 1, of which waited for: 1 -> 0; matrix products, arithmetic and copies ran while one was open for 3% -> 4% of each run, Pallas kernels for 0% -> 14%
where the time goes in v7:
time: 222 us; the launch traced here: 220 us
  blocking collectives  109 us (49%)
  Pallas kernels  79.3 us (36%)
  local copies, waits for them, and re-layouts  20.9 us (9%)
  other arithmetic  9.23 us (4%)
    all_to_all x1, blocking collectives, shards(): got = lax.all_to_all(spec, ('wide', 'narrow'), 0, 0, tiled=True)  109 us
    pallas_call x2, Pallas kernels, pfb_chunk(): pl.pallas_call(functools.partial(spectra_kernel, with_halo), out_shape=ja...  61.9 us
    pallas_call x1, Pallas kernels, visibilities(): pl.pallas_call(functools.partial(gram_kernel, n_narrow), out_shape=jax.Sh...  17.4 us
    reshape x1, local copies, waits for them, and re-layouts, shards(): out = out.reshape(steps, PHASES, 2, c1_len, local_inputs, CHUNK)  9.18 us
    unnamed x3, local copies, waits for them, and re-layouts  8.77 us
  transfers between devices with their start and end apart: 1, of which 0 were waited for; matrix products, arithmetic and copies ran while one was open for 4% of the time, Pallas kernels for 14%

profile of v7, /device:TPU:1, one launch (start us, length us, event | category | flops | bytes accessed | tf_op | source)
XLA Modules:
  0.0 219.9 jit_solution(14463039266115430898)
XLA Ops:
  0.0 1.9 slice.3
  1.9 1.3 collective-permute-start
  3.2 0.6 fusion.14
  3.8 4.2 %fusion.9 = (f32[8,256,128]{2,1,0:T(8,128)S(1)}, f32[8,256,128]{2,1,0:T(8,128)S(1)}, f32[8,256,128]{2,1,0:T(8,128)S(1)}) fusion(s32[8,128]{1,0:T(8,128)S(1)} %iota_add_fusion), kind=kLoop, calls=%fused_computation.18 | loop fusion | flops 4456448 | bytes 3149824 | tf_op jit(solution)/shard_map/neg | solution.py:42
  8.0 2.5 %fusion.2 = (bf16[8,512,256]{2,1,0:T(8,128)(2,1)}, bf16[8,512,256]{2,1,0:T(8,128)(2,1)}) fusion(f32[8,256,128]{2,1,0:T(8,128)S(1)} %get-tuple-element.9, f32[8,256,128]{2,1,0:T(8,128)S(1)} %get-tuple-element.8, f32[8,256,128]{2,1,0:T(8,128)S(1)} %get-tuple-element.7), kind=kLoop, calls=%fused_computation.4 | loop fusion | flops 9437184 | bytes 7340032 | tf_op jit(solution)/shard_map/convert_element_type | solution.py:52
  10.5 1.1 broadcast_in_dim.15.refs_1_.refs_2_
  11.6 0.0 copy-start
  11.6 30.9 %shard_map.28.refs_5_ = bf16[2,8,256,1024]{3,2,1,0:T(8,128)(2,1)} custom-call(bf16[8,524288]{1,0:T(8,128)(2,1)} %refs_0_.3, f32[16,8,2048]{2,1,0:T(8,128)} %broadcast_in_dim.15.refs_1_.refs_2_, bf16[8,512,256]{2,1,0:T(8,128)(2,1)} %get-tuple-element.6.refs_2_.refs_3_, bf16[8,512,256]{2,1,0:T(8,128)(2,1)} %get-tuple-element.5.refs_3_.refs_4_), custom_call_target="tpu_custom_call" | custom-call | flops 5704253440 | bytes 13074432 | tf_op jit(solution)/shard_map/pallas_call | solution.py:184
  42.5 0.0 collective-permute-done
  42.5 0.0 copy-done
  42.5 1.9 broadcast_select_fusion.refs_1_
  44.4 31.0 %shard_map.29 = bf16[2,8,256,1024]{3,2,1,0:T(8,128)(2,1)} custom-call(bf16[8,524288]{1,0:T(8,128)(2,1)} %refs_0_.3, bf16[8,30720]{1,0:T(8,128)(2,1)} %broadcast_select_fusion.refs_1_, f32[16,8,2048]{2,1,0:T(8,128)} %broadcast_in_dim.15.refs_1_.refs_2_, bf16[8,512,256]{2,1,0:T(8,128)(2,1)} %get-tuple-element.6.refs_2_.refs_3_, ...), custom_call_target="tpu_custom_call", output_to_operand_aliasing={{}: (5, {})} | custom-call | flops 5704253440 | bytes 12582912 | tf_op jit(solution)/shard_map/pallas_call | solution.py:184
  75.4 8.8 %copy.5 = bf16[512,8,8,128]{3,2,1,0:T(8,128)(2,1)} copy(bf16[512,8,8,128]{3,1,2,0:T(8,128)(2,1)} %bitcast.8) | data formatting | bytes 16777216
  84.2 9.2 %copy.7 = bf16[2,8,2,128,8,128]{5,4,0,2,1,3:T(8,128)(2,1)} copy(bf16[2,8,2,128,8,128]{5,4,3,2,1,0:T(8,128)(2,1)} %bitcast.9) | data formatting | bytes 16777216 | tf_op jit(solution)/shard_map/reshape | solution.py:273
  93.4 109.2 %all_to_all.5.g_ref = bf16[128,8,2,2,8,128]{5,4,3,2,1,0:T(8,128)(2,1)} all-to-all(bf16[128,8,2,2,8,128]{5,4,3,2,1,0:T(8,128)(2,1)} %bitcast.10), channel_id=1, replica_groups=mesh['wide'=64,'narrow'=2] {'wide','narrow'}, dimensions={0} | all-to-all | bytes 16777216 | tf_op jit(solution)/shard_map/all_to_all | solution.py:275
  202.5 17.4 %shard_map.30 = f32[8,2,512,512]{3,2,1,0:T(8,128)} custom-call(bf16[128,8,2,2,8,128]{5,4,3,2,1,0:T(8,128)(2,1)} %all_to_all.5.g_ref), custom_call_target="tpu_custom_call" | custom-call | flops 8589934592 | bytes 25165824 | tf_op jit(solution)/shard_map/pallas_call | solution.py:240
  (2 shorter events, 0.0 us)
Async XLA Ops:
  1.9 40.6 %collective-permute-start = (bf16[8,30720]{1,0:T(8,128)(2,1)}, bf16[8,30720]{1,0:T(8,128)(2,1)}, u32[]{:S(2)}, u32[]{:S(2)}) collective-permute-start(bf16[8,30720]{1,0:T(8,128)(2,1)} %slice.3), channel_id=1, source_target_pairs={{1,0},{3,2},{5,4},{7,6},{9,8},{11,10},{13,12},{15,14},{17,16},{19,... | collective-permute-start | bytes 1474568 | tf_op jit(solution)/shard_map/ppermute | solution.py:22
  11.6 30.9 %copy-start = (bf16[8,30720]{1,0:T(8,128)(2,1)S(1)}, bf16[8,30720]{1,0:T(8,128)(2,1)}, u32[]{:S(2)}) copy-start(bf16[8,30720]{1,0:T(8,128)(2,1)} %param.3) | copy-start | bytes 1474564

commit v8 on v7

--- a/solution.py
+++ b/solution.py
@@ -208,6 +208,49 @@
     return pfb_chunk(xa, xh, wb, bh, bl, steps - 1, first)
 
 
+def exchange_kernel(n_narrow, src_ref, dst_ref, send_sem, recv_sem, own_sem):
+    n_dev = src_ref.shape[0]
+    me = lax.axis_index("wide") * n_narrow + lax.axis_index("narrow")
+    own = pltpu.make_async_copy(src_ref.at[me], dst_ref.at[me], own_sem)
+    own.start()
+
+    def send(k, _):
+        peer = lax.rem(me + k, n_dev)
+        pltpu.make_async_remote_copy(
+            src_ref=src_ref.at[peer],
+            dst_ref=dst_ref.at[me],
+            send_sem=send_sem,
+            recv_sem=recv_sem,
+            device_id=(peer // n_narrow, peer % n_narrow),
+            device_id_type=pl.DeviceIdType.MESH,
+        ).start()
+        return 0
+
+    lax.fori_loop(1, n_dev, send, 0)
+    own.wait()
+    every = pltpu.make_async_remote_copy(
+        src_ref=src_ref.at[pl.ds(0, n_dev - 1)],
+        dst_ref=dst_ref.at[pl.ds(0, n_dev - 1)],
+        send_sem=send_sem,
+        recv_sem=recv_sem,
+        device_id=(0, 0),
+        device_id_type=pl.DeviceIdType.MESH,
+    )
+    every.wait_send()
+    every.wait_recv()
+
+
+def exchange(spec, n_narrow):
+    return pl.pallas_call(
+        functools.partial(exchange_kernel, n_narrow),
+        out_shape=jax.ShapeDtypeStruct(spec.shape, spec.dtype),
+        in_specs=[pl.BlockSpec(memory_space=pl.ANY)],
+        out_specs=pl.BlockSpec(memory_space=pl.ANY),
+        scratch_shapes=[pltpu.SemaphoreType.DMA(()), pltpu.SemaphoreType.DMA(()), pltpu.SemaphoreType.DMA(())],
+        compiler_params=pltpu.CompilerParams(has_side_effects=True),
+    )(spec)
+
+
 def gram_kernel(n_narrow, g_ref, out_ref, l_ref):
     n_src = g_ref.shape[0]
     steps = g_ref.shape[3]
@@ -272,7 +315,7 @@
     c1_len = CHANNELS // PHASES
     out = out.reshape(steps, PHASES, 2, c1_len, local_inputs, CHUNK)
     spec = jnp.transpose(out, (3, 1, 2, 0, 4, 5))
-    got = lax.all_to_all(spec, ("wide", "narrow"), 0, 0, tiled=True)
+    got = exchange(spec, lax.axis_size("narrow"))
     return visibilities(got, lax.axis_size("narrow"))
 
 

time: 222 us -> 273 us (1.23)
  Pallas kernels: 79.3 us -> 241 us
  blocking collectives: 109 us -> 0 us
    pallas_call x0 -> x1, Pallas kernels: none -> 162 us  [exchange(): pl.pallas_call(functools.partial(exchange_kernel, n_narrow), out_shape=ja...]
    all_to_all x1 -> x0, blocking collectives: 109 us -> none  [shards(): got = lax.all_to_all(spec, ('wide', 'narrow'), 0, 0, tiled=True)]
  transfers between devices with their start and end apart: 1 -> 1, of which waited for: 0 -> 0; matrix products, arithmetic and copies ran while one was open for 4% -> 3% of each run, Pallas kernels for 14% -> 11%
where the time goes in v8:
time: 273 us; the launch traced here: 272 us
  Pallas kernels  241 us (88%)
  local copies, waits for them, and re-layouts  20.9 us (8%)
  other arithmetic  9.23 us (3%)
    pallas_call x1, Pallas kernels, exchange(): pl.pallas_call(functools.partial(exchange_kernel, n_narrow), out_shape=ja...  162 us
    pallas_call x2, Pallas kernels, pfb_chunk(): pl.pallas_call(functools.partial(spectra_kernel, with_halo), out_shape=ja...  61.9 us
    pallas_call x1, Pallas kernels, visibilities(): pl.pallas_call(functools.partial(gram_kernel, n_narrow), out_shape=jax.Sh...  17.4 us
    reshape x1, local copies, waits for them, and re-layouts, shards(): out = out.reshape(steps, PHASES, 2, c1_len, local_inputs, CHUNK)  9.18 us
    unnamed x3, local copies, waits for them, and re-layouts  8.77 us
  transfers between devices with their start and end apart: 1, of which 0 were waited for; matrix products, arithmetic and copies ran while one was open for 3% of the time, Pallas kernels for 11%

profile of v8, /device:TPU:1, one launch (start us, length us, event | category | flops | bytes accessed | tf_op | source)
XLA Modules:
  0.0 272.3 jit_solution(2132998406769252172)
XLA Ops:
  0.0 1.9 slice.3
  1.9 1.3 collective-permute-start
  3.2 0.6 fusion.14
  3.8 4.2 %fusion.9 = (f32[8,256,128]{2,1,0:T(8,128)S(1)}, f32[8,256,128]{2,1,0:T(8,128)S(1)}, f32[8,256,128]{2,1,0:T(8,128)S(1)}) fusion(s32[8,128]{1,0:T(8,128)S(1)} %iota_add_fusion), kind=kLoop, calls=%fused_computation.18 | loop fusion | flops 4456448 | bytes 3149824 | tf_op jit(solution)/shard_map/neg | solution.py:42
  8.0 2.5 fusion.2
  10.5 1.1 broadcast_in_dim.15.refs_1_.refs_2_
  11.6 0.0 copy-start
  11.6 30.9 %shard_map.28.refs_5_ = bf16[2,8,256,1024]{3,2,1,0:T(8,128)(2,1)} custom-call(bf16[8,524288]{1,0:T(8,128)(2,1)} %refs_0_.3, f32[16,8,2048]{2,1,0:T(8,128)} %broadcast_in_dim.15.refs_1_.refs_2_, bf16[8,512,256]{2,1,0:T(8,128)(2,1)} %get-tuple-element.6.refs_2_.refs_3_, bf16[8,512,256]{2,1,0:T(8,128)(2,1)} %get-tuple-element.5.refs_3_.refs_4_), custom_call_target="tpu_custom_call" | custom-call | flops 5704253440 | bytes 13074432 | tf_op jit(solution)/shard_map/pallas_call | solution.py:184
  42.5 0.0 collective-permute-done
  42.5 0.0 copy-done
  42.5 1.9 broadcast_select_fusion.refs_1_
  44.4 31.0 %shard_map.29 = bf16[2,8,256,1024]{3,2,1,0:T(8,128)(2,1)} custom-call(bf16[8,524288]{1,0:T(8,128)(2,1)} %refs_0_.3, bf16[8,30720]{1,0:T(8,128)(2,1)} %broadcast_select_fusion.refs_1_, f32[16,8,2048]{2,1,0:T(8,128)} %broadcast_in_dim.15.refs_1_.refs_2_, bf16[8,512,256]{2,1,0:T(8,128)(2,1)} %get-tuple-element.6.refs_2_.refs_3_, ...), custom_call_target="tpu_custom_call", output_to_operand_aliasing={{}: (5, {})} | custom-call | flops 5704253440 | bytes 12582912 | tf_op jit(solution)/shard_map/pallas_call | solution.py:184
  75.4 8.8 %copy.5 = bf16[512,8,8,128]{3,2,1,0:T(8,128)(2,1)} copy(bf16[512,8,8,128]{3,1,2,0:T(8,128)(2,1)} %bitcast.8) | data formatting | bytes 16777216
  84.2 9.2 %copy.7 = bf16[2,8,2,128,8,128]{5,4,0,2,1,3:T(8,128)(2,1)} copy(bf16[2,8,2,128,8,128]{5,4,3,2,1,0:T(8,128)(2,1)} %bitcast.9) | data formatting | bytes 16777216 | tf_op jit(solution)/shard_map/reshape | solution.py:316
  93.4 161.6 %shard_map.30.g_ref = bf16[128,8,2,2,8,128]{5,4,3,2,1,0:T(8,128)(2,1)} custom-call(bf16[128,8,2,2,8,128]{5,4,3,2,1,0:T(8,128)(2,1)} %bitcast.10), custom_call_target="tpu_custom_call" | custom-call | tf_op jit(solution)/shard_map/pallas_call | solution.py:244
  254.9 17.4 %shard_map.31 = f32[8,2,512,512]{3,2,1,0:T(8,128)} custom-call(bf16[128,8,2,2,8,128]{5,4,3,2,1,0:T(8,128)(2,1)} %shard_map.30.g_ref), custom_call_target="tpu_custom_call" | custom-call | flops 8589934592 | bytes 25165824 | tf_op jit(solution)/shard_map/pallas_call | solution.py:283
  (2 shorter events, 0.0 us)
Async XLA Ops:
  1.9 40.6 %collective-permute-start = (bf16[8,30720]{1,0:T(8,128)(2,1)}, bf16[8,30720]{1,0:T(8,128)(2,1)}, u32[]{:S(2)}, u32[]{:S(2)}) collective-permute-start(bf16[8,30720]{1,0:T(8,128)(2,1)} %slice.3), channel_id=1, source_target_pairs={{1,0},{3,2},{5,4},{7,6},{9,8},{11,10},{13,12},{15,14},{17,16},{19,... | collective-permute-start | bytes 1474568 | tf_op jit(solution)/shard_map/ppermute | solution.py:22
  11.6 30.9 %copy-start = (bf16[8,30720]{1,0:T(8,128)(2,1)S(1)}, bf16[8,30720]{1,0:T(8,128)(2,1)}, u32[]{:S(2)}) copy-start(bf16[8,30720]{1,0:T(8,128)(2,1)} %param.3) | copy-start | bytes 1474564

commit v9 on v7

--- a/solution.py
+++ b/solution.py
@@ -31,14 +31,20 @@
 
 
 def phase_matrices(salt):
-    k1 = jnp.arange(SUB_LEN, dtype=jnp.int32)[None, :, None]
     c1 = jnp.arange(CHANNELS // PHASES, dtype=jnp.int32)[None, None, :] + salt
     c2 = jnp.arange(PHASES, dtype=jnp.int32)[:, None, None]
-    turns = (k1 * (PHASES * c1 + c2)) % FFT_LEN
-    angles = (2.0 * jnp.pi / FFT_LEN) * turns.astype(jnp.float32)
+    chan = PHASES * c1 + c2
+    step = 16
+    a = jnp.arange(SUB_LEN // step, dtype=jnp.int32)[None, :, None]
+    b = jnp.arange(step, dtype=jnp.int32)[None, :, None]
+    coarse = (2.0 * jnp.pi / FFT_LEN) * ((a * step * chan) % FFT_LEN).astype(jnp.float32)
+    fine = (2.0 * jnp.pi / FFT_LEN) * ((b * chan) % FFT_LEN).astype(jnp.float32)
+    cc, sc = jnp.cos(coarse)[:, :, None, :], jnp.sin(coarse)[:, :, None, :]
+    cf, sf = jnp.cos(fine)[:, None, :, :], jnp.sin(fine)[:, None, :, :]
     scaling = 1.0 / math.sqrt(FFT_LEN)
-    cos_t = jnp.cos(angles) * scaling
-    sin_t = jnp.sin(angles) * scaling
+    shape = (PHASES, SUB_LEN, CHANNELS // PHASES)
+    cos_t = ((cc * cf - sc * sf) * scaling).reshape(shape)
+    sin_t = ((sc * cf + cc * sf) * scaling).reshape(shape)
     top = jnp.concatenate([cos_t, -sin_t], axis=-1)
     bottom = jnp.concatenate([sin_t, cos_t], axis=-1)
     full = jnp.concatenate([top, bottom], axis=1)
@@ -72,14 +78,14 @@
         xf_ref[q_local] = xa_ref[:, pl.ds(start, FFT_LEN)].astype(jnp.float32)
         return 0
 
-    lax.fori_loop(0, own, load_block, 0)
+    lax.fori_loop(0, own, load_block, 0, unroll=4)
 
     if with_halo:
         def body(j, _):
             start = pl.multiple_of(j * FFT_LEN, FFT_LEN)
             xf_ref[CHUNK + j] = xh_ref[:, pl.ds(start, FFT_LEN)].astype(jnp.float32)
             return 0
-        lax.fori_loop(0, TAPS - 1, body, 0)
+        lax.fori_loop(0, TAPS - 1, body, 0, unroll=3)
 
     lane_w = 128
     for lane_at in range(FFT_LEN // lane_w):

time: 222 us -> 217 us (0.977)
  other arithmetic: 9.23 us -> 5.8 us
    neg x1, other arithmetic: 4.17 us -> 0.07 us  [phase_matrices(): top = jnp.concatenate([cos_t, -sin_t], axis=-1)]
  transfers between devices with their start and end apart: 1 -> 1, of which waited for: 0 -> 0; matrix products, arithmetic and copies ran while one was open for 4% -> 2% of each run, Pallas kernels for 14% -> 14%
where the time goes in v9:
time: 217 us; the launch traced here: 216 us
  blocking collectives  109 us (50%)
  Pallas kernels  78.4 us (36%)
  local copies, waits for them, and re-layouts  20.9 us (10%)
  other arithmetic  5.8 us (3%)
    all_to_all x1, blocking collectives, shards(): got = lax.all_to_all(spec, ('wide', 'narrow'), 0, 0, tiled=True)  109 us
    pallas_call x2, Pallas kernels, pfb_chunk(): pl.pallas_call(functools.partial(spectra_kernel, with_halo), out_shape=ja...  61 us
    pallas_call x1, Pallas kernels, visibilities(): pl.pallas_call(functools.partial(gram_kernel, n_narrow), out_shape=jax.Sh...  17.3 us
    reshape x1, local copies, waits for them, and re-layouts, shards(): out = out.reshape(steps, PHASES, 2, c1_len, local_inputs, CHUNK)  9.18 us
    unnamed x3, local copies, waits for them, and re-layouts  8.77 us
  transfers between devices with their start and end apart: 1, of which 0 were waited for; matrix products, arithmetic and copies ran while one was open for 2% of the time, Pallas kernels for 14%

profile of v9, /device:TPU:1, one launch (start us, length us, event | category | flops | bytes accessed | tf_op | source)
XLA Modules:
  0.0 215.6 jit_solution(3945371189450529870)
XLA Ops:
  0.0 1.9 slice.3
  1.9 1.3 collective-permute-start
  3.2 0.6 fusion.7
  3.8 0.5 fusion.28
  4.4 0.3 add_multiply_fusion
  4.7 0.1 bitcast_negate_fusion
  4.7 2.4 %fusion.2 = (bf16[8,512,256]{2,1,0:T(8,128)(2,1)}, bf16[8,512,256]{2,1,0:T(8,128)(2,1)}) fusion(f32[8,256,128]{2,1,0:T(8,128)S(1)} %bitcast.15, f32[8,256,128]{2,1,0:T(8,128)S(1)} %bitcast.14, f32[8,256,128]{2,1,0:T(8,128)S(1)} %bitcast_negate_fusion), kind=kLoop, calls=%fused_computation.4 | loop fusion | flops 9437184 | bytes 7340032 | tf_op jit(solution)/shard_map/convert_element_type | solution.py:58
  7.1 1.1 broadcast_in_dim.9.refs_1_.refs_2_
  8.2 0.0 copy-start
  8.2 30.4 %shard_map.28.refs_5_ = bf16[2,8,256,1024]{3,2,1,0:T(8,128)(2,1)} custom-call(bf16[8,524288]{1,0:T(8,128)(2,1)} %refs_0_.3, f32[16,8,2048]{2,1,0:T(8,128)} %broadcast_in_dim.9.refs_1_.refs_2_, bf16[8,512,256]{2,1,0:T(8,128)(2,1)} %get-tuple-element.6.refs_2_.refs_3_, bf16[8,512,256]{2,1,0:T(8,128)(2,1)} %get-tuple-element.5.refs_3_.refs_4_), custom_call_target="tpu_custom_call" | custom-call | flops 5704253440 | bytes 13074432 | tf_op jit(solution)/shard_map/pallas_call | solution.py:190
  38.6 0.0 collective-permute-done
  38.6 0.0 copy-done
  38.6 1.9 broadcast_select_fusion.refs_1_
  40.5 30.6 %shard_map.29 = bf16[2,8,256,1024]{3,2,1,0:T(8,128)(2,1)} custom-call(bf16[8,524288]{1,0:T(8,128)(2,1)} %refs_0_.3, bf16[8,30720]{1,0:T(8,128)(2,1)} %broadcast_select_fusion.refs_1_, f32[16,8,2048]{2,1,0:T(8,128)} %broadcast_in_dim.9.refs_1_.refs_2_, bf16[8,512,256]{2,1,0:T(8,128)(2,1)} %get-tuple-element.6.refs_2_.refs_3_, ...), custom_call_target="tpu_custom_call", output_to_operand_aliasing={{}: (5, {})} | custom-call | flops 5704253440 | bytes 12582912 | tf_op jit(solution)/shard_map/pallas_call | solution.py:190
  71.1 8.8 %copy.5 = bf16[512,8,8,128]{3,2,1,0:T(8,128)(2,1)} copy(bf16[512,8,8,128]{3,1,2,0:T(8,128)(2,1)} %bitcast.11) | data formatting | bytes 16777216
  79.9 9.2 %copy.7 = bf16[2,8,2,128,8,128]{5,4,0,2,1,3:T(8,128)(2,1)} copy(bf16[2,8,2,128,8,128]{5,4,3,2,1,0:T(8,128)(2,1)} %bitcast.12) | data formatting | bytes 16777216 | tf_op jit(solution)/shard_map/reshape | solution.py:279
  89.1 109.2 %all_to_all.5.g_ref = bf16[128,8,2,2,8,128]{5,4,3,2,1,0:T(8,128)(2,1)} all-to-all(bf16[128,8,2,2,8,128]{5,4,3,2,1,0:T(8,128)(2,1)} %bitcast.13), channel_id=1, replica_groups=mesh['wide'=64,'narrow'=2] {'wide','narrow'}, dimensions={0} | all-to-all | bytes 16777216 | tf_op jit(solution)/shard_map/all_to_all | solution.py:281
  198.2 17.3 %shard_map.30 = f32[8,2,512,512]{3,2,1,0:T(8,128)} custom-call(bf16[128,8,2,2,8,128]{5,4,3,2,1,0:T(8,128)(2,1)} %all_to_all.5.g_ref), custom_call_target="tpu_custom_call" | custom-call | flops 8589934592 | bytes 25165824 | tf_op jit(solution)/shard_map/pallas_call | solution.py:246
  (3 shorter events, 0.0 us)
Async XLA Ops:
  1.9 36.8 %collective-permute-start = (bf16[8,30720]{1,0:T(8,128)(2,1)}, bf16[8,30720]{1,0:T(8,128)(2,1)}, u32[]{:S(2)}, u32[]{:S(2)}) collective-permute-start(bf16[8,30720]{1,0:T(8,128)(2,1)} %slice.3), channel_id=1, source_target_pairs={{1,0},{3,2},{5,4},{7,6},{9,8},{11,10},{13,12},{15,14},{17,16},{19,... | collective-permute-start | bytes 1474568 | tf_op jit(solution)/shard_map/ppermute | solution.py:22
  8.2 30.4 %copy-start = (bf16[8,30720]{1,0:T(8,128)(2,1)S(1)}, bf16[8,30720]{1,0:T(8,128)(2,1)}, u32[]{:S(2)}) copy-start(bf16[8,30720]{1,0:T(8,128)(2,1)} %param.3) | copy-start | bytes 1474564

commit v10 on v9

--- a/solution.py
+++ b/solution.py
@@ -66,10 +66,9 @@
 
 def spectra_kernel(with_halo, *refs):
     if with_halo:
-        xa_ref, xh_ref, wb_ref, bh_ref, bl_ref, _, out_ref, xf_ref, f_ref, uh_ref, ul_ref = refs
+        xa_ref, fol_ref, sh_ref, wb_ref, bh_ref, bl_ref, _, out_ref, xf_ref, f_ref, uh_ref, ul_ref = refs
     else:
         xa_ref, wb_ref, bh_ref, bl_ref, out_ref, xf_ref, f_ref, uh_ref, ul_ref = refs
-        xh_ref = xa_ref
     n_in = xa_ref.shape[0]
     own = CHUNK if with_halo else CHUNK + TAPS - 1
 
@@ -81,9 +80,13 @@
     lax.fori_loop(0, own, load_block, 0, unroll=4)
 
     if with_halo:
+        is_final = lax.axis_index("narrow") == lax.axis_size("narrow") - 1
+
         def body(j, _):
             start = pl.multiple_of(j * FFT_LEN, FFT_LEN)
-            xf_ref[CHUNK + j] = xh_ref[:, pl.ds(start, FFT_LEN)].astype(jnp.float32)
+            lanes = pl.ds(start, FFT_LEN)
+            picked = jnp.where(is_final, fol_ref[:, lanes], sh_ref[:, lanes])
+            xf_ref[CHUNK + j] = picked.astype(jnp.float32)
             return 0
         lax.fori_loop(0, TAPS - 1, body, 0, unroll=3)
 
@@ -176,8 +179,9 @@
     in_specs = [pl.BlockSpec(xa_spec.block_shape, xa_spec.index_map, pipeline_mode=pl.Buffered(1))]
     operands = [xa]
     if with_halo:
-        in_specs.append(pl.BlockSpec(xh.shape, lambda s: (0, 0), pipeline_mode=pl.Buffered(1)))
-        operands.append(xh)
+        for arr in xh:
+            in_specs.append(pl.BlockSpec(arr.shape, lambda s: (0, 0), pipeline_mode=pl.Buffered(1)))
+            operands.append(arr)
     for arr in (wb, bh, bl):
         in_specs.append(pl.BlockSpec(arr.shape, const3, pipeline_mode=pl.Buffered(1)))
         operands.append(arr)
@@ -267,8 +271,7 @@
     halo_len = (TAPS - 1) * FFT_LEN
     leading = voltages[:, :halo_len]
     shifted = from_behind(leading, "narrow", -1)
-    is_final = lax.axis_index("narrow") == lax.axis_size("narrow") - 1
-    after_rows = jnp.where(is_final, following, shifted)
+    after_rows = (following, shifted)
     weights_taps = pfb_window(FFT_LEN, TAPS).reshape(TAPS, 1, FFT_LEN)
     wb = jnp.broadcast_to(weights_taps, (TAPS, local_inputs, FFT_LEN))
     salt = lax.optimization_barrier(jnp.zeros((), jnp.int32))

time: 217 us -> 216 us (level)
  no operation moved by 1% of the time
where the time goes in v10:
time: 216 us; the launch traced here: 214 us
  blocking collectives  109 us (50%)
  Pallas kernels  78.5 us (36%)
  local copies, waits for them, and re-layouts  20.9 us (10%)
  other arithmetic  3.95 us (2%)
    all_to_all x1, blocking collectives, shards(): got = lax.all_to_all(spec, ('wide', 'narrow'), 0, 0, tiled=True)  109 us
    pallas_call x2, Pallas kernels, pfb_chunk(): pl.pallas_call(functools.partial(spectra_kernel, with_halo), out_shape=ja...  61.1 us
    pallas_call x1, Pallas kernels, visibilities(): pl.pallas_call(functools.partial(gram_kernel, n_narrow), out_shape=jax.Sh...  17.4 us
    unnamed x3, local copies, waits for them, and re-layouts  9.58 us
    reshape x1, local copies, waits for them, and re-layouts, shards(): out = out.reshape(steps, PHASES, 2, c1_len, local_inputs, CHUNK)  9.18 us
  transfers between devices with their start and end apart: 1, of which 0 were waited for; matrix products, arithmetic and copies ran while one was open for 2% of the time, Pallas kernels for 14%

profile of v10, /device:TPU:1, one launch (start us, length us, event | category | flops | bytes accessed | tf_op | source)
XLA Modules:
  0.0 214.1 jit_solution(10875986918727345700)
XLA Ops:
  0.0 1.1 slice.3
  1.1 1.3 collective-permute-start
  2.4 0.6 fusion.7
  3.0 0.5 fusion.28
  3.6 0.3 add_multiply_fusion
  3.9 0.1 bitcast_negate_fusion
  3.9 2.4 %fusion.2 = (bf16[8,512,256]{2,1,0:T(8,128)(2,1)}, bf16[8,512,256]{2,1,0:T(8,128)(2,1)}) fusion(f32[8,256,128]{2,1,0:T(8,128)S(1)} %bitcast.15, f32[8,256,128]{2,1,0:T(8,128)S(1)} %bitcast.14, f32[8,256,128]{2,1,0:T(8,128)S(1)} %bitcast_negate_fusion), kind=kLoop, calls=%fused_computation.4 | loop fusion | flops 9437184 | bytes 7340032 | tf_op jit(solution)/shard_map/convert_element_type | solution.py:58
  6.4 1.1 broadcast_in_dim.9.refs_1_.refs_3_
  7.4 30.4 %shard_map.28.refs_6_ = bf16[2,8,256,1024]{3,2,1,0:T(8,128)(2,1)} custom-call(bf16[8,524288]{1,0:T(8,128)(2,1)} %refs_0_.3, f32[16,8,2048]{2,1,0:T(8,128)} %broadcast_in_dim.9.refs_1_.refs_3_, bf16[8,512,256]{2,1,0:T(8,128)(2,1)} %get-tuple-element.6.refs_2_.refs_4_, bf16[8,512,256]{2,1,0:T(8,128)(2,1)} %get-tuple-element.5.refs_3_.refs_5_), custom_call_target="tpu_custom_call" | custom-call | flops 5704253440 | bytes 13074432 | tf_op jit(solution)/shard_map/pallas_call | solution.py:194
  37.8 0.0 collective-permute-done.refs_2_
  37.8 0.0 copy-start
  37.8 0.8 copy-done
  38.7 30.7 %shard_map.29 = bf16[2,8,256,1024]{3,2,1,0:T(8,128)(2,1)} custom-call(bf16[8,524288]{1,0:T(8,128)(2,1)} %refs_0_.3, bf16[8,30720]{1,0:T(8,128)(2,1)} %refs_1_.1, bf16[8,30720]{1,0:T(8,128)(2,1)} %copy-done, f32[16,8,2048]{2,1,0:T(8,128)} %broadcast_in_dim.9.refs_1_.refs_3_, ...), custom_call_target="tpu_custom_call", output_to_operand_aliasing={{}: (6, {})} | custom-call | flops 5704253440 | bytes 12582912 | tf_op jit(solution)/shard_map/pallas_call | solution.py:194
  69.4 8.8 %copy.5 = bf16[512,8,8,128]{3,2,1,0:T(8,128)(2,1)} copy(bf16[512,8,8,128]{3,1,2,0:T(8,128)(2,1)} %bitcast.11) | data formatting | bytes 16777216
  78.2 9.2 %copy.7 = bf16[2,8,2,128,8,128]{5,4,0,2,1,3:T(8,128)(2,1)} copy(bf16[2,8,2,128,8,128]{5,4,3,2,1,0:T(8,128)(2,1)} %bitcast.12) | data formatting | bytes 16777216 | tf_op jit(solution)/shard_map/reshape | solution.py:282
  87.3 109.4 %all_to_all.5.g_ref = bf16[128,8,2,2,8,128]{5,4,3,2,1,0:T(8,128)(2,1)} all-to-all(bf16[128,8,2,2,8,128]{5,4,3,2,1,0:T(8,128)(2,1)} %bitcast.13), channel_id=1, replica_groups=mesh['wide'=64,'narrow'=2] {'wide','narrow'}, dimensions={0} | all-to-all | bytes 16777216 | tf_op jit(solution)/shard_map/all_to_all | solution.py:284
  196.8 17.4 %shard_map.30 = f32[8,2,512,512]{3,2,1,0:T(8,128)} custom-call(bf16[128,8,2,2,8,128]{5,4,3,2,1,0:T(8,128)(2,1)} %all_to_all.5.g_ref), custom_call_target="tpu_custom_call" | custom-call | flops 8589934592 | bytes 25165824 | tf_op jit(solution)/shard_map/pallas_call | solution.py:250
  (3 shorter events, 0.0 us)
Async XLA Ops:
  1.1 36.8 %collective-permute-start = (bf16[8,30720]{1,0:T(8,128)(2,1)S(1)}, bf16[8,30720]{1,0:T(8,128)(2,1)S(1)}, u32[]{:S(2)}, u32[]{:S(2)}) collective-permute-start(bf16[8,30720]{1,0:T(8,128)(2,1)S(1)} %slice.3), channel_id=1, source_target_pairs={{1,0},{3,2},{5,4},{7,6},{9,8},{11,10},{13,12},{15,14},{17,16},{19,... | collective-permute-start | bytes 1474568 | tf_op jit(solution)/shard_map/ppermute | solution.py:22
  37.8 0.8 copy-start

commit v11 on v10

--- a/solution.py
+++ b/solution.py
@@ -234,13 +234,14 @@
         return 0
 
     lax.fori_loop(0, n_src // n_narrow, gather, 0)
-    both = l_ref[...].astype(jnp.bfloat16)
+    rows = l_ref[...]
+    both = rows.astype(jnp.bfloat16)
+    both_t = rows.T.astype(jnp.bfloat16)
     half = both.shape[1] // 2
     turned = jnp.concatenate([both[:, half:], -both[:, :half]], axis=1)
-    nt = (((1,), (1,)), ((), ()))
     scale = 1.0 / half
-    out_ref[0, 0] = lax.dot_general(both, both, nt, preferred_element_type=jnp.float32) * scale
-    out_ref[0, 1] = lax.dot_general(turned, both, nt, preferred_element_type=jnp.float32) * scale
+    out_ref[0, 0] = jnp.dot(both, both_t, preferred_element_type=jnp.float32) * scale
+    out_ref[0, 1] = jnp.dot(turned, both_t, preferred_element_type=jnp.float32) * scale
 
 
 def visibilities(got, n_narrow):

time: 216 us -> 216 us (level)
  no operation moved by 1% of the time
where the time goes in v11:
time: 216 us; the launch traced here: 215 us
  blocking collectives  109 us (50%)
  Pallas kernels  79.1 us (37%)
  local copies, waits for them, and re-layouts  20.9 us (10%)
  other arithmetic  3.95 us (2%)
    all_to_all x1, blocking collectives, shards(): got = lax.all_to_all(spec, ('wide', 'narrow'), 0, 0, tiled=True)  109 us
    pallas_call x2, Pallas kernels, pfb_chunk(): pl.pallas_call(functools.partial(spectra_kernel, with_halo), out_shape=ja...  61.1 us
    pallas_call x1, Pallas kernels, visibilities(): pl.pallas_call(functools.partial(gram_kernel, n_narrow), out_shape=jax.Sh...  17.9 us
    unnamed x3, local copies, waits for them, and re-layouts  9.58 us
    reshape x1, local copies, waits for them, and re-layouts, shards(): out = out.reshape(steps, PHASES, 2, c1_len, local_inputs, CHUNK)  9.18 us
  transfers between devices with their start and end apart: 1, of which 0 were waited for; matrix products, arithmetic and copies ran while one was open for 2% of the time, Pallas kernels for 14%

profile of v11, /device:TPU:1, one launch (start us, length us, event | category | flops | bytes accessed | tf_op | source)
XLA Modules:
  0.0 214.7 jit_solution(10877281261459384238)
XLA Ops:
  0.0 1.1 slice.3
  1.1 1.3 collective-permute-start
  2.4 0.6 fusion.7
  3.0 0.5 fusion.28
  3.6 0.3 add_multiply_fusion
  3.9 0.1 bitcast_negate_fusion
  3.9 2.4 %fusion.2 = (bf16[8,512,256]{2,1,0:T(8,128)(2,1)}, bf16[8,512,256]{2,1,0:T(8,128)(2,1)}) fusion(f32[8,256,128]{2,1,0:T(8,128)S(1)} %bitcast.15, f32[8,256,128]{2,1,0:T(8,128)S(1)} %bitcast.14, f32[8,256,128]{2,1,0:T(8,128)S(1)} %bitcast_negate_fusion), kind=kLoop, calls=%fused_computation.4 | loop fusion | flops 9437184 | bytes 7340032 | tf_op jit(solution)/shard_map/convert_element_type | solution.py:58
  6.4 1.1 broadcast_in_dim.9.refs_1_.refs_3_
  7.4 30.4 %shard_map.28.refs_6_ = bf16[2,8,256,1024]{3,2,1,0:T(8,128)(2,1)} custom-call(bf16[8,524288]{1,0:T(8,128)(2,1)} %refs_0_.3, f32[16,8,2048]{2,1,0:T(8,128)} %broadcast_in_dim.9.refs_1_.refs_3_, bf16[8,512,256]{2,1,0:T(8,128)(2,1)} %get-tuple-element.6.refs_2_.refs_4_, bf16[8,512,256]{2,1,0:T(8,128)(2,1)} %get-tuple-element.5.refs_3_.refs_5_), custom_call_target="tpu_custom_call" | custom-call | flops 5704253440 | bytes 13074432 | tf_op jit(solution)/shard_map/pallas_call | solution.py:194
  37.8 0.0 collective-permute-done.refs_2_
  37.8 0.0 copy-start
  37.8 0.8 copy-done
  38.7 30.7 %shard_map.29 = bf16[2,8,256,1024]{3,2,1,0:T(8,128)(2,1)} custom-call(bf16[8,524288]{1,0:T(8,128)(2,1)} %refs_0_.3, bf16[8,30720]{1,0:T(8,128)(2,1)} %refs_1_.1, bf16[8,30720]{1,0:T(8,128)(2,1)} %copy-done, f32[16,8,2048]{2,1,0:T(8,128)} %broadcast_in_dim.9.refs_1_.refs_3_, ...), custom_call_target="tpu_custom_call", output_to_operand_aliasing={{}: (6, {})} | custom-call | flops 5704253440 | bytes 12582912 | tf_op jit(solution)/shard_map/pallas_call | solution.py:194
  69.4 8.8 %copy.5 = bf16[512,8,8,128]{3,2,1,0:T(8,128)(2,1)} copy(bf16[512,8,8,128]{3,1,2,0:T(8,128)(2,1)} %bitcast.11) | data formatting | bytes 16777216
  78.2 9.2 %copy.7 = bf16[2,8,2,128,8,128]{5,4,0,2,1,3:T(8,128)(2,1)} copy(bf16[2,8,2,128,8,128]{5,4,3,2,1,0:T(8,128)(2,1)} %bitcast.12) | data formatting | bytes 16777216 | tf_op jit(solution)/shard_map/reshape | solution.py:283
  87.3 109.4 %all_to_all.5.g_ref = bf16[128,8,2,2,8,128]{5,4,3,2,1,0:T(8,128)(2,1)} all-to-all(bf16[128,8,2,2,8,128]{5,4,3,2,1,0:T(8,128)(2,1)} %bitcast.13), channel_id=1, replica_groups=mesh['wide'=64,'narrow'=2] {'wide','narrow'}, dimensions={0} | all-to-all | bytes 16777216 | tf_op jit(solution)/shard_map/all_to_all | solution.py:285
  196.8 17.9 %shard_map.30 = f32[8,2,512,512]{3,2,1,0:T(8,128)} custom-call(bf16[128,8,2,2,8,128]{5,4,3,2,1,0:T(8,128)(2,1)} %all_to_all.5.g_ref), custom_call_target="tpu_custom_call" | custom-call | flops 8589934592 | bytes 25165824 | tf_op jit(solution)/shard_map/pallas_call | solution.py:251
  (3 shorter events, 0.0 us)
Async XLA Ops:
  1.1 36.8 %collective-permute-start = (bf16[8,30720]{1,0:T(8,128)(2,1)S(1)}, bf16[8,30720]{1,0:T(8,128)(2,1)S(1)}, u32[]{:S(2)}, u32[]{:S(2)}) collective-permute-start(bf16[8,30720]{1,0:T(8,128)(2,1)S(1)} %slice.3), channel_id=1, source_target_pairs={{1,0},{3,2},{5,4},{7,6},{9,8},{11,10},{13,12},{15,14},{17,16},{19,... | collective-permute-start | bytes 1474568 | tf_op jit(solution)/shard_map/ppermute | solution.py:22
  37.8 0.8 copy-start

commit v12 on v10

--- a/solution.py
+++ b/solution.py
@@ -153,7 +153,7 @@
                         ul_ref[c2, ls, im_l] = lo
             return 0
 
-        lax.fori_loop(0, sub_rows // rows_per, butterflies, 0)
+        lax.fori_loop(0, sub_rows // rows_per, butterflies, 0, unroll=2)
 
         for c2 in range(PHASES):
             depth = SUB_LEN if c2 in (0, PHASES // 2) else 2 * SUB_LEN
@@ -233,7 +233,7 @@
                     l_ref[pl.ds(row, n_in), col:col + seg] = g_ref[w * n_narrow + n, 0, ri, s].astype(jnp.float32)
         return 0
 
-    lax.fori_loop(0, n_src // n_narrow, gather, 0)
+    lax.fori_loop(0, n_src // n_narrow, gather, 0, unroll=2)
     both = l_ref[...].astype(jnp.bfloat16)
     half = both.shape[1] // 2
     turned = jnp.concatenate([both[:, half:], -both[:, :half]], axis=1)

time: 216 us -> 215 us (level)
  no operation moved by 1% of the time
where the time goes in v12:
time: 215 us; the launch traced here: 213 us
  blocking collectives  109 us (51%)
  Pallas kernels  77.3 us (36%)
  local copies, waits for them, and re-layouts  20.9 us (10%)
  other arithmetic  3.95 us (2%)
    all_to_all x1, blocking collectives, shards(): got = lax.all_to_all(spec, ('wide', 'narrow'), 0, 0, tiled=True)  109 us
    pallas_call x2, Pallas kernels, pfb_chunk(): pl.pallas_call(functools.partial(spectra_kernel, with_halo), out_shape=ja...  60.8 us
    pallas_call x1, Pallas kernels, visibilities(): pl.pallas_call(functools.partial(gram_kernel, n_narrow), out_shape=jax.Sh...  16.5 us
    unnamed x3, local copies, waits for them, and re-layouts  9.58 us
    reshape x1, local copies, waits for them, and re-layouts, shards(): out = out.reshape(steps, PHASES, 2, c1_len, local_inputs, CHUNK)  9.18 us
  transfers between devices with their start and end apart: 1, of which 0 were waited for; matrix products, arithmetic and copies ran while one was open for 2% of the time, Pallas kernels for 14%

profile of v12, /device:TPU:1, one launch (start us, length us, event | category | flops | bytes accessed | tf_op | source)
XLA Modules:
  0.0 212.9 jit_solution(15228581116366881798)
XLA Ops:
  0.0 1.1 slice.3
  1.1 1.3 collective-permute-start
  2.4 0.6 fusion.7
  3.0 0.5 fusion.28
  3.6 0.3 add_multiply_fusion
  3.9 0.1 bitcast_negate_fusion
  3.9 2.4 %fusion.2 = (bf16[8,512,256]{2,1,0:T(8,128)(2,1)}, bf16[8,512,256]{2,1,0:T(8,128)(2,1)}) fusion(f32[8,256,128]{2,1,0:T(8,128)S(1)} %bitcast.15, f32[8,256,128]{2,1,0:T(8,128)S(1)} %bitcast.14, f32[8,256,128]{2,1,0:T(8,128)S(1)} %bitcast_negate_fusion), kind=kLoop, calls=%fused_computation.4 | loop fusion | flops 9437184 | bytes 7340032 | tf_op jit(solution)/shard_map/convert_element_type | solution.py:58
  6.4 1.1 broadcast_in_dim.9.refs_1_.refs_3_
  7.4 30.2 %shard_map.28.refs_6_ = bf16[2,8,256,1024]{3,2,1,0:T(8,128)(2,1)} custom-call(bf16[8,524288]{1,0:T(8,128)(2,1)} %refs_0_.3, f32[16,8,2048]{2,1,0:T(8,128)} %broadcast_in_dim.9.refs_1_.refs_3_, bf16[8,512,256]{2,1,0:T(8,128)(2,1)} %get-tuple-element.6.refs_2_.refs_4_, bf16[8,512,256]{2,1,0:T(8,128)(2,1)} %get-tuple-element.5.refs_3_.refs_5_), custom_call_target="tpu_custom_call" | custom-call | flops 5704253440 | bytes 13074432 | tf_op jit(solution)/shard_map/pallas_call | solution.py:194
  37.7 0.0 collective-permute-done.refs_2_
  37.7 0.0 copy-start
  37.7 0.8 copy-done
  38.5 30.6 %shard_map.29 = bf16[2,8,256,1024]{3,2,1,0:T(8,128)(2,1)} custom-call(bf16[8,524288]{1,0:T(8,128)(2,1)} %refs_0_.3, bf16[8,30720]{1,0:T(8,128)(2,1)} %refs_1_.1, bf16[8,30720]{1,0:T(8,128)(2,1)} %copy-done, f32[16,8,2048]{2,1,0:T(8,128)} %broadcast_in_dim.9.refs_1_.refs_3_, ...), custom_call_target="tpu_custom_call", output_to_operand_aliasing={{}: (6, {})} | custom-call | flops 5704253440 | bytes 12582912 | tf_op jit(solution)/shard_map/pallas_call | solution.py:194
  69.0 8.8 %copy.5 = bf16[512,8,8,128]{3,2,1,0:T(8,128)(2,1)} copy(bf16[512,8,8,128]{3,1,2,0:T(8,128)(2,1)} %bitcast.11) | data formatting | bytes 16777216
  77.8 9.2 %copy.7 = bf16[2,8,2,128,8,128]{5,4,0,2,1,3:T(8,128)(2,1)} copy(bf16[2,8,2,128,8,128]{5,4,3,2,1,0:T(8,128)(2,1)} %bitcast.12) | data formatting | bytes 16777216 | tf_op jit(solution)/shard_map/reshape | solution.py:282
  87.0 109.4 %all_to_all.5.g_ref = bf16[128,8,2,2,8,128]{5,4,3,2,1,0:T(8,128)(2,1)} all-to-all(bf16[128,8,2,2,8,128]{5,4,3,2,1,0:T(8,128)(2,1)} %bitcast.13), channel_id=1, replica_groups=mesh['wide'=64,'narrow'=2] {'wide','narrow'}, dimensions={0} | all-to-all | bytes 16777216 | tf_op jit(solution)/shard_map/all_to_all | solution.py:284
  196.4 16.5 %shard_map.30 = f32[8,2,512,512]{3,2,1,0:T(8,128)} custom-call(bf16[128,8,2,2,8,128]{5,4,3,2,1,0:T(8,128)(2,1)} %all_to_all.5.g_ref), custom_call_target="tpu_custom_call" | custom-call | flops 8589934592 | bytes 25165824 | tf_op jit(solution)/shard_map/pallas_call | solution.py:250
  (3 shorter events, 0.0 us)
Async XLA Ops:
  1.1 36.6 %collective-permute-start = (bf16[8,30720]{1,0:T(8,128)(2,1)S(1)}, bf16[8,30720]{1,0:T(8,128)(2,1)S(1)}, u32[]{:S(2)}, u32[]{:S(2)}) collective-permute-start(bf16[8,30720]{1,0:T(8,128)(2,1)S(1)} %slice.3), channel_id=1, source_target_pairs={{1,0},{3,2},{5,4},{7,6},{9,8},{11,10},{13,12},{15,14},{17,16},{19,... | collective-permute-start | bytes 1474568 | tf_op jit(solution)/shard_map/ppermute | solution.py:22
  37.7 0.8 copy-start

commit v13 on v12

--- a/solution.py
+++ b/solution.py
@@ -102,7 +102,7 @@
             f_ref[lane_at, pl.ds(ml, n_in, stride=CHUNK), :] = terms[0]
             return 0
 
-        lax.fori_loop(0, CHUNK, filt, 0, unroll=4)
+        lax.fori_loop(0, CHUNK, filt, 0, unroll=8)
 
     half = 1.0 / math.sqrt(2.0)
     rows_per = 16
@@ -233,7 +233,7 @@
                     l_ref[pl.ds(row, n_in), col:col + seg] = g_ref[w * n_narrow + n, 0, ri, s].astype(jnp.float32)
         return 0
 
-    lax.fori_loop(0, n_src // n_narrow, gather, 0, unroll=2)
+    lax.fori_loop(0, n_src // n_narrow, gather, 0, unroll=4)
     both = l_ref[...].astype(jnp.bfloat16)
     half = both.shape[1] // 2
     turned = jnp.concatenate([both[:, half:], -both[:, :half]], axis=1)

time: 215 us -> 210 us (0.977)
  Pallas kernels: 77.3 us -> 72.6 us
    pallas_call x2, Pallas kernels: 60.8 us -> 56.4 us  [pfb_chunk(): pl.pallas_call(functools.partial(spectra_kernel, with_halo), out_shape=ja...]
  transfers between devices with their start and end apart: 1 -> 1, of which waited for: 0 -> 0; matrix products, arithmetic and copies ran while one was open for 2% -> 2% of each run, Pallas kernels for 14% -> 13%
where the time goes in v13:
time: 210 us; the launch traced here: 208 us
  blocking collectives  109 us (52%)
  Pallas kernels  72.6 us (35%)
  local copies, waits for them, and re-layouts  20.9 us (10%)
  other arithmetic  3.95 us (2%)
    all_to_all x1, blocking collectives, shards(): got = lax.all_to_all(spec, ('wide', 'narrow'), 0, 0, tiled=True)  109 us
    pallas_call x2, Pallas kernels, pfb_chunk(): pl.pallas_call(functools.partial(spectra_kernel, with_halo), out_shape=ja...  56.4 us
    pallas_call x1, Pallas kernels, visibilities(): pl.pallas_call(functools.partial(gram_kernel, n_narrow), out_shape=jax.Sh...  16.2 us
    unnamed x3, local copies, waits for them, and re-layouts  9.58 us
    reshape x1, local copies, waits for them, and re-layouts, shards(): out = out.reshape(steps, PHASES, 2, c1_len, local_inputs, CHUNK)  9.18 us
  transfers between devices with their start and end apart: 1, of which 0 were waited for; matrix products, arithmetic and copies ran while one was open for 2% of the time, Pallas kernels for 13%

profile of v13, /device:TPU:1, one launch (start us, length us, event | category | flops | bytes accessed | tf_op | source)
XLA Modules:
  0.0 208.3 jit_solution(2207377085893075097)
XLA Ops:
  0.0 1.1 slice.3
  1.1 1.3 collective-permute-start
  2.4 0.6 fusion.7
  3.0 0.5 fusion.28
  3.6 0.3 add_multiply_fusion
  3.9 0.1 bitcast_negate_fusion
  3.9 2.4 %fusion.2 = (bf16[8,512,256]{2,1,0:T(8,128)(2,1)}, bf16[8,512,256]{2,1,0:T(8,128)(2,1)}) fusion(f32[8,256,128]{2,1,0:T(8,128)S(1)} %bitcast.15, f32[8,256,128]{2,1,0:T(8,128)S(1)} %bitcast.14, f32[8,256,128]{2,1,0:T(8,128)S(1)} %bitcast_negate_fusion), kind=kLoop, calls=%fused_computation.4 | loop fusion | flops 9437184 | bytes 7340032 | tf_op jit(solution)/shard_map/convert_element_type | solution.py:58
  6.4 1.1 broadcast_in_dim.9.refs_1_.refs_3_
  7.4 28.0 %shard_map.28.refs_6_ = bf16[2,8,256,1024]{3,2,1,0:T(8,128)(2,1)} custom-call(bf16[8,524288]{1,0:T(8,128)(2,1)} %refs_0_.3, f32[16,8,2048]{2,1,0:T(8,128)} %broadcast_in_dim.9.refs_1_.refs_3_, bf16[8,512,256]{2,1,0:T(8,128)(2,1)} %get-tuple-element.6.refs_2_.refs_4_, bf16[8,512,256]{2,1,0:T(8,128)(2,1)} %get-tuple-element.5.refs_3_.refs_5_), custom_call_target="tpu_custom_call" | custom-call | flops 5704253440 | bytes 13074432 | tf_op jit(solution)/shard_map/pallas_call | solution.py:194
  35.5 0.0 collective-permute-done.refs_2_
  35.5 0.0 copy-start
  35.5 0.8 copy-done
  36.3 28.4 %shard_map.29 = bf16[2,8,256,1024]{3,2,1,0:T(8,128)(2,1)} custom-call(bf16[8,524288]{1,0:T(8,128)(2,1)} %refs_0_.3, bf16[8,30720]{1,0:T(8,128)(2,1)} %refs_1_.1, bf16[8,30720]{1,0:T(8,128)(2,1)} %copy-done, f32[16,8,2048]{2,1,0:T(8,128)} %broadcast_in_dim.9.refs_1_.refs_3_, ...), custom_call_target="tpu_custom_call", output_to_operand_aliasing={{}: (6, {})} | custom-call | flops 5704253440 | bytes 12582912 | tf_op jit(solution)/shard_map/pallas_call | solution.py:194
  64.7 8.8 %copy.5 = bf16[512,8,8,128]{3,2,1,0:T(8,128)(2,1)} copy(bf16[512,8,8,128]{3,1,2,0:T(8,128)(2,1)} %bitcast.11) | data formatting | bytes 16777216
  73.5 9.2 %copy.7 = bf16[2,8,2,128,8,128]{5,4,0,2,1,3:T(8,128)(2,1)} copy(bf16[2,8,2,128,8,128]{5,4,3,2,1,0:T(8,128)(2,1)} %bitcast.12) | data formatting | bytes 16777216 | tf_op jit(solution)/shard_map/reshape | solution.py:282
  82.6 109.4 %all_to_all.5.g_ref = bf16[128,8,2,2,8,128]{5,4,3,2,1,0:T(8,128)(2,1)} all-to-all(bf16[128,8,2,2,8,128]{5,4,3,2,1,0:T(8,128)(2,1)} %bitcast.13), channel_id=1, replica_groups=mesh['wide'=64,'narrow'=2] {'wide','narrow'}, dimensions={0} | all-to-all | bytes 16777216 | tf_op jit(solution)/shard_map/all_to_all | solution.py:284
  192.1 16.2 %shard_map.30 = f32[8,2,512,512]{3,2,1,0:T(8,128)} custom-call(bf16[128,8,2,2,8,128]{5,4,3,2,1,0:T(8,128)(2,1)} %all_to_all.5.g_ref), custom_call_target="tpu_custom_call" | custom-call | flops 8589934592 | bytes 25165824 | tf_op jit(solution)/shard_map/pallas_call | solution.py:250
  (3 shorter events, 0.0 us)
Async XLA Ops:
  1.1 34.4 %collective-permute-start = (bf16[8,30720]{1,0:T(8,128)(2,1)S(1)}, bf16[8,30720]{1,0:T(8,128)(2,1)S(1)}, u32[]{:S(2)}, u32[]{:S(2)}) collective-permute-start(bf16[8,30720]{1,0:T(8,128)(2,1)S(1)} %slice.3), channel_id=1, source_target_pairs={{1,0},{3,2},{5,4},{7,6},{9,8},{11,10},{13,12},{15,14},{17,16},{19,... | collective-permute-start | bytes 1474568 | tf_op jit(solution)/shard_map/ppermute | solution.py:22
  35.5 0.8 copy-start

commit v14 on v13

--- a/solution.py
+++ b/solution.py
@@ -102,7 +102,7 @@
             f_ref[lane_at, pl.ds(ml, n_in, stride=CHUNK), :] = terms[0]
             return 0
 
-        lax.fori_loop(0, CHUNK, filt, 0, unroll=8)
+        lax.fori_loop(0, CHUNK, filt, 0, unroll=16)
 
     half = 1.0 / math.sqrt(2.0)
     rows_per = 16

time: 210 us -> 208 us (level)
    pallas_call x2, Pallas kernels: 56.4 us -> 54.3 us  [pfb_chunk(): pl.pallas_call(functools.partial(spectra_kernel, with_halo), out_shape=ja...]
where the time goes in v14:
time: 208 us; the launch traced here: 206 us
  blocking collectives  109 us (52%)
  Pallas kernels  70.5 us (34%)
  local copies, waits for them, and re-layouts  20.9 us (10%)
  other arithmetic  3.95 us (2%)
    all_to_all x1, blocking collectives, shards(): got = lax.all_to_all(spec, ('wide', 'narrow'), 0, 0, tiled=True)  109 us
    pallas_call x2, Pallas kernels, pfb_chunk(): pl.pallas_call(functools.partial(spectra_kernel, with_halo), out_shape=ja...  54.3 us
    pallas_call x1, Pallas kernels, visibilities(): pl.pallas_call(functools.partial(gram_kernel, n_narrow), out_shape=jax.Sh...  16.2 us
    unnamed x3, local copies, waits for them, and re-layouts  9.58 us
    reshape x1, local copies, waits for them, and re-layouts, shards(): out = out.reshape(steps, PHASES, 2, c1_len, local_inputs, CHUNK)  9.18 us
  transfers between devices with their start and end apart: 1, of which 0 were waited for; matrix products, arithmetic and copies ran while one was open for 2% of the time, Pallas kernels for 13%

profile of v14, /device:TPU:1, one launch (start us, length us, event | category | flops | bytes accessed | tf_op | source)
XLA Modules:
  0.0 206.1 jit_solution(16586744590782048643)
XLA Ops:
  0.0 1.1 slice.3
  1.1 1.3 collective-permute-start
  2.4 0.6 fusion.7
  3.0 0.5 fusion.28
  3.6 0.3 add_multiply_fusion
  3.9 0.1 bitcast_negate_fusion
  3.9 2.4 %fusion.2 = (bf16[8,512,256]{2,1,0:T(8,128)(2,1)}, bf16[8,512,256]{2,1,0:T(8,128)(2,1)}) fusion(f32[8,256,128]{2,1,0:T(8,128)S(1)} %bitcast.15, f32[8,256,128]{2,1,0:T(8,128)S(1)} %bitcast.14, f32[8,256,128]{2,1,0:T(8,128)S(1)} %bitcast_negate_fusion), kind=kLoop, calls=%fused_computation.4 | loop fusion | flops 9437184 | bytes 7340032 | tf_op jit(solution)/shard_map/convert_element_type | solution.py:58
  6.4 1.1 broadcast_in_dim.9.refs_1_.refs_3_
  7.4 27.0 %shard_map.28.refs_6_ = bf16[2,8,256,1024]{3,2,1,0:T(8,128)(2,1)} custom-call(bf16[8,524288]{1,0:T(8,128)(2,1)} %refs_0_.3, f32[16,8,2048]{2,1,0:T(8,128)} %broadcast_in_dim.9.refs_1_.refs_3_, bf16[8,512,256]{2,1,0:T(8,128)(2,1)} %get-tuple-element.6.refs_2_.refs_4_, bf16[8,512,256]{2,1,0:T(8,128)(2,1)} %get-tuple-element.5.refs_3_.refs_5_), custom_call_target="tpu_custom_call" | custom-call | flops 5704253440 | bytes 13074432 | tf_op jit(solution)/shard_map/pallas_call | solution.py:194
  34.4 0.0 collective-permute-done.refs_2_
  34.4 0.0 copy-start
  34.4 0.8 copy-done
  35.2 27.3 %shard_map.29 = bf16[2,8,256,1024]{3,2,1,0:T(8,128)(2,1)} custom-call(bf16[8,524288]{1,0:T(8,128)(2,1)} %refs_0_.3, bf16[8,30720]{1,0:T(8,128)(2,1)} %refs_1_.1, bf16[8,30720]{1,0:T(8,128)(2,1)} %copy-done, f32[16,8,2048]{2,1,0:T(8,128)} %broadcast_in_dim.9.refs_1_.refs_3_, ...), custom_call_target="tpu_custom_call", output_to_operand_aliasing={{}: (6, {})} | custom-call | flops 5704253440 | bytes 12582912 | tf_op jit(solution)/shard_map/pallas_call | solution.py:194
  62.5 8.8 %copy.5 = bf16[512,8,8,128]{3,2,1,0:T(8,128)(2,1)} copy(bf16[512,8,8,128]{3,1,2,0:T(8,128)(2,1)} %bitcast.11) | data formatting | bytes 16777216
  71.3 9.2 %copy.7 = bf16[2,8,2,128,8,128]{5,4,0,2,1,3:T(8,128)(2,1)} copy(bf16[2,8,2,128,8,128]{5,4,3,2,1,0:T(8,128)(2,1)} %bitcast.12) | data formatting | bytes 16777216 | tf_op jit(solution)/shard_map/reshape | solution.py:282
  80.5 109.5 %all_to_all.5.g_ref = bf16[128,8,2,2,8,128]{5,4,3,2,1,0:T(8,128)(2,1)} all-to-all(bf16[128,8,2,2,8,128]{5,4,3,2,1,0:T(8,128)(2,1)} %bitcast.13), channel_id=1, replica_groups=mesh['wide'=64,'narrow'=2] {'wide','narrow'}, dimensions={0} | all-to-all | bytes 16777216 | tf_op jit(solution)/shard_map/all_to_all | solution.py:284
  189.9 16.2 %shard_map.30 = f32[8,2,512,512]{3,2,1,0:T(8,128)} custom-call(bf16[128,8,2,2,8,128]{5,4,3,2,1,0:T(8,128)(2,1)} %all_to_all.5.g_ref), custom_call_target="tpu_custom_call" | custom-call | flops 8589934592 | bytes 25165824 | tf_op jit(solution)/shard_map/pallas_call | solution.py:250
  (3 shorter events, 0.0 us)
Async XLA Ops:
  1.1 33.4 %collective-permute-start = (bf16[8,30720]{1,0:T(8,128)(2,1)S(1)}, bf16[8,30720]{1,0:T(8,128)(2,1)S(1)}, u32[]{:S(2)}, u32[]{:S(2)}) collective-permute-start(bf16[8,30720]{1,0:T(8,128)(2,1)S(1)} %slice.3), channel_id=1, source_target_pairs={{1,0},{3,2},{5,4},{7,6},{9,8},{11,10},{13,12},{15,14},{17,16},{19,... | collective-permute-start | bytes 1474568 | tf_op jit(solution)/shard_map/ppermute | solution.py:22
  34.4 0.8 copy-start

commit v15 on v14

--- a/solution.py
+++ b/solution.py
@@ -153,7 +153,7 @@
                         ul_ref[c2, ls, im_l] = lo
             return 0
 
-        lax.fori_loop(0, sub_rows // rows_per, butterflies, 0, unroll=2)
+        lax.fori_loop(0, sub_rows // rows_per, butterflies, 0, unroll=4)
 
         for c2 in range(PHASES):
             depth = SUB_LEN if c2 in (0, PHASES // 2) else 2 * SUB_LEN

time: 208 us -> 208 us (level)
  no operation moved by 1% of the time
where the time goes in v15:
time: 208 us; the launch traced here: 206 us
  blocking collectives  109 us (52%)
  Pallas kernels  70.2 us (34%)
  local copies, waits for them, and re-layouts  20.9 us (10%)
  other arithmetic  3.95 us (2%)
    all_to_all x1, blocking collectives, shards(): got = lax.all_to_all(spec, ('wide', 'narrow'), 0, 0, tiled=True)  109 us
    pallas_call x2, Pallas kernels, pfb_chunk(): pl.pallas_call(functools.partial(spectra_kernel, with_halo), out_shape=ja...  54 us
    pallas_call x1, Pallas kernels, visibilities(): pl.pallas_call(functools.partial(gram_kernel, n_narrow), out_shape=jax.Sh...  16.2 us
    unnamed x3, local copies, waits for them, and re-layouts  9.58 us
    reshape x1, local copies, waits for them, and re-layouts, shards(): out = out.reshape(steps, PHASES, 2, c1_len, local_inputs, CHUNK)  9.18 us
  transfers between devices with their start and end apart: 1, of which 0 were waited for; matrix products, arithmetic and copies ran while one was open for 2% of the time, Pallas kernels for 13%

profile of v15, /device:TPU:1, one launch (start us, length us, event | category | flops | bytes accessed | tf_op | source)
XLA Modules:
  0.0 205.9 jit_solution(8477595399201052500)
XLA Ops:
  0.0 1.1 slice.3
  1.1 1.3 collective-permute-start
  2.4 0.6 fusion.7
  3.0 0.5 fusion.28
  3.6 0.3 add_multiply_fusion
  3.9 0.1 bitcast_negate_fusion
  3.9 2.4 %fusion.2 = (bf16[8,512,256]{2,1,0:T(8,128)(2,1)}, bf16[8,512,256]{2,1,0:T(8,128)(2,1)}) fusion(f32[8,256,128]{2,1,0:T(8,128)S(1)} %bitcast.15, f32[8,256,128]{2,1,0:T(8,128)S(1)} %bitcast.14, f32[8,256,128]{2,1,0:T(8,128)S(1)} %bitcast_negate_fusion), kind=kLoop, calls=%fused_computation.4 | loop fusion | flops 9437184 | bytes 7340032 | tf_op jit(solution)/shard_map/convert_element_type | solution.py:58
  6.4 1.1 broadcast_in_dim.9.refs_1_.refs_3_
  7.4 26.8 %shard_map.28.refs_6_ = bf16[2,8,256,1024]{3,2,1,0:T(8,128)(2,1)} custom-call(bf16[8,524288]{1,0:T(8,128)(2,1)} %refs_0_.3, f32[16,8,2048]{2,1,0:T(8,128)} %broadcast_in_dim.9.refs_1_.refs_3_, bf16[8,512,256]{2,1,0:T(8,128)(2,1)} %get-tuple-element.6.refs_2_.refs_4_, bf16[8,512,256]{2,1,0:T(8,128)(2,1)} %get-tuple-element.5.refs_3_.refs_5_), custom_call_target="tpu_custom_call" | custom-call | flops 5704253440 | bytes 13074432 | tf_op jit(solution)/shard_map/pallas_call | solution.py:194
  34.3 0.0 collective-permute-done.refs_2_
  34.3 0.0 copy-start
  34.3 0.8 copy-done
  35.1 27.2 %shard_map.29 = bf16[2,8,256,1024]{3,2,1,0:T(8,128)(2,1)} custom-call(bf16[8,524288]{1,0:T(8,128)(2,1)} %refs_0_.3, bf16[8,30720]{1,0:T(8,128)(2,1)} %refs_1_.1, bf16[8,30720]{1,0:T(8,128)(2,1)} %copy-done, f32[16,8,2048]{2,1,0:T(8,128)} %broadcast_in_dim.9.refs_1_.refs_3_, ...), custom_call_target="tpu_custom_call", output_to_operand_aliasing={{}: (6, {})} | custom-call | flops 5704253440 | bytes 12582912 | tf_op jit(solution)/shard_map/pallas_call | solution.py:194
  62.3 8.8 %copy.5 = bf16[512,8,8,128]{3,2,1,0:T(8,128)(2,1)} copy(bf16[512,8,8,128]{3,1,2,0:T(8,128)(2,1)} %bitcast.11) | data formatting | bytes 16777216
  71.0 9.2 %copy.7 = bf16[2,8,2,128,8,128]{5,4,0,2,1,3:T(8,128)(2,1)} copy(bf16[2,8,2,128,8,128]{5,4,3,2,1,0:T(8,128)(2,1)} %bitcast.12) | data formatting | bytes 16777216 | tf_op jit(solution)/shard_map/reshape | solution.py:282
  80.2 109.4 %all_to_all.5.g_ref = bf16[128,8,2,2,8,128]{5,4,3,2,1,0:T(8,128)(2,1)} all-to-all(bf16[128,8,2,2,8,128]{5,4,3,2,1,0:T(8,128)(2,1)} %bitcast.13), channel_id=1, replica_groups=mesh['wide'=64,'narrow'=2] {'wide','narrow'}, dimensions={0} | all-to-all | bytes 16777216 | tf_op jit(solution)/shard_map/all_to_all | solution.py:284
  189.7 16.2 %shard_map.30 = f32[8,2,512,512]{3,2,1,0:T(8,128)} custom-call(bf16[128,8,2,2,8,128]{5,4,3,2,1,0:T(8,128)(2,1)} %all_to_all.5.g_ref), custom_call_target="tpu_custom_call" | custom-call | flops 8589934592 | bytes 25165824 | tf_op jit(solution)/shard_map/pallas_call | solution.py:250
  (3 shorter events, 0.0 us)
Async XLA Ops:
  1.1 33.2 %collective-permute-start = (bf16[8,30720]{1,0:T(8,128)(2,1)S(1)}, bf16[8,30720]{1,0:T(8,128)(2,1)S(1)}, u32[]{:S(2)}, u32[]{:S(2)}) collective-permute-start(bf16[8,30720]{1,0:T(8,128)(2,1)S(1)} %slice.3), channel_id=1, source_target_pairs={{1,0},{3,2},{5,4},{7,6},{9,8},{11,10},{13,12},{15,14},{17,16},{19,... | collective-permute-start | bytes 1474568 | tf_op jit(solution)/shard_map/ppermute | solution.py:22
  34.3 0.8 copy-start
